TPU v7x, 512 devices: a whole 4x8x8 slice. The times are simulated.
512 devices in a mesh: parts: 512 (over x, y, z, core).
Axes of the slice: x: 4, y: 8, z: 8, core: 2. Of those that a mesh axis runs over, the one named last changes fastest.
Arguments:
- flow_state: float32 [5, 64, 32768], P(None, None, 'parts'), may hold values from -2 to 14, as said below
- state_tangent: float32 [5, 64, 32768], P(None, None, 'parts'), may hold values from -6 to 6
- far_field: float32 [5], replicated, may hold values from -0.3 to 5, as said below
- coordinates: float32 [3, 52224], P(None, 'parts'), as said below
- damping: float32 [2], replicated, may hold values from 0.1 to 1
- face_neighbour: int32 [6, 32768], P(None, 'parts'), may hold values from 0 to 96, as said below
- element_nodes: int32 [8, 32768], P(None, 'parts'), may hold values from 0 to 152, as said below
- upper_sends: int32 [16384], P('parts'), may hold values from 0 to 63, as said below
- lower_sends: int32 [16384], P('parts'), may hold values from 0 to 63, as said below
- node_sends: int32 [26112], P('parts'), may hold values from 0 to 101, as said below
- shock_flags: int32 [32768], P('parts'), may hold values from 0 to 1, as said below
Outputs:
- residual: float32 [5, 64, 32768], P(None, None, 'parts')
- state_change: float32 [5, 64, 32768], P(None, None, 'parts')
- node_update: float32 [3, 52224], P(None, 'parts')
Inputs may be any that keep to these rules, and one draw needn't show every extreme that they name: `flow_state`: density and pressure at each point lie in 0.5 to 2 and velocity components within 1 of (0, 0, 1.5). `far_field`: density and pressure lie in 0.8 to 1.2, velocity components within 0.2 of (0, 0, 1.5). `coordinates`: hexahedra stay valid: each element's trilinear map keeps a positive Jacobian at all points. `face_neighbour`: entry f of an element is a local element below 64, 64 + a halo slot below 32 (faces 0 and 1 only), or 96 for the far field; neighbours share the element's reference orientation. `element_nodes`: a local owned node below 102, or 102 + a halo slot of a node owned by the next partition. `upper_sends`: on each partition 32 distinct local elements. `lower_sends`: on each partition 32 distinct local elements. `node_sends`: on each partition 51 distinct owned nodes. `shock_flags`: at most 16 flagged elements in one partition, and some partition has exactly 16.
All inputs are finite; a program needn't handle non-finite values.
Results may differ from a plain program's by a relative error of at most 0.0003.
Values sent between devices are 32-bit elements; how exact they have to be, the bound alone decides.
No kernel may reach another device: no remote copies, remote signals or barrier semaphores. Data moves between devices by JAX's collectives and lax.ppermute only.
A program may use at most 128 MiB of HBM per device.

v0:
```python
import functools
import math

import jax
import jax.numpy as jnp
import numpy as np
from jax import lax
from jax.experimental import pallas as pl
from jax.experimental.pallas import tpu as pltpu
from jax.sharding import PartitionSpec as P

GAMMA = 1.4
SOFTENING = 0.01
HIGHEST = lax.Precision.HIGHEST
F32 = jnp.float32


def lobatto_tables():
    points = np.array([-1.0, -math.sqrt(0.2), math.sqrt(0.2), 1.0])
    weights = np.array([1.0, 5.0, 5.0, 1.0]) / 6.0
    derivative = np.zeros((4, 4))
    for a in range(4):
        for b in range(4):
            if a == b:
                derivative[a, b] = sum((1.0 / (points[a] - points[m]) for m in range(4) if m != a))
            else:
                numerator = 1.0
                denominator = 1.0
                for m in range(4):
                    if m != b:
                        denominator *= points[b] - points[m]
                        if m != a:
                            numerator *= points[a] - points[m]
                derivative[a, b] = numerator / denominator
    return (points, weights, derivative)


def shape_gradients():
    points = lobatto_tables()[0]
    gradients = np.zeros((3, 64, 8))
    for q in range(64):
        position = (q // 16, q // 4 % 4, q % 4)
        for k in range(8):
            corner_bits = (k // 4, k // 2 % 2, k % 2)
            for j in range(3):
                factor = 1.0
                for m in range(3):
                    orient = 1.0 if corner_bits[m] == 1 else -1.0
                    if m == j:
                        factor *= 0.5 * orient
                    else:
                        factor *= 0.5 * (1.0 + orient * points[position[m]])
                gradients[j, q, k] = factor
    return gradients


def edge_laplacian():
    matrix = np.zeros((8, 8))
    for k in range(8):
        matrix[k, k] = 3.0
        for b in range(3):
            matrix[k, k ^ 1 << b] = -1.0
    return matrix


def face_rows(j, s):
    rows = [q for q in range(64) if (q // 16, q // 4 % 4, q % 4)[j] == 3 * s]
    return np.array(rows)


def constant_matrices():
    points, weights, derivative = lobatto_tables()
    volume = np.einsum("a,b,c->abc", weights, weights, weights).reshape(64)
    face = np.einsum("a,b->ab", weights, weights).reshape(16)
    eye = np.eye(4)
    full = [
        np.kron(np.kron(derivative, eye), eye),
        np.kron(np.kron(eye, derivative), eye),
        np.kron(np.kron(eye, eye), derivative),
    ]
    assemble = np.zeros((128, 144))
    for half in range(2):
        rows = slice(64 * half, 64 * half + 64)
        for j in range(3):
            weighted = volume[:, None] * full[j]
            assemble[rows, 32 * j : 32 * j + 32] = weighted[:, 32 * half : 32 * half + 32]
            for point, q in enumerate(face_rows(j, half)):
                assemble[64 * half + q, 96 + 16 * j + point] = face[point]
    gradients = shape_gradients()
    corner = np.zeros((200, 16))
    for half in range(2):
        columns = slice(8 * half, 8 * half + 8)
        for j in range(3):
            corner[32 * j : 32 * j + 32, columns] = gradients[j, 32 * half : 32 * half + 32]
            for which in range(2):
                base = 96 + 48 * which + 16 * j
                corner[base : base + 16, columns] = gradients[(j + 1 + which) % 3][
                    face_rows(j, half)
                ]
    corner[192:200, 0:8] = edge_laplacian()
    return assemble.astype(np.float32), corner.astype(np.float32)


def dot(a, b):
    return jnp.dot(a, b, precision=HIGHEST, preferred_element_type=F32)


def dot_transposed(a, b):
    return lax.dot_general(
        a, b, (((1,), (1,)), ((), ())), precision=HIGHEST, preferred_element_type=F32
    )


def lanes(rows=8):
    return lax.broadcasted_iota(jnp.int32, (rows, 128), 1)


def pair(left, right):
    return jnp.concatenate([left, right], axis=1)


def pick(table, index):
    blocks = [
        jnp.take_along_axis(table[r : r + 8], index, axis=1, mode="promise_in_bounds")
        for r in range(0, table.shape[0], 8)
    ]
    return blocks[0] if len(blocks) == 1 else jnp.concatenate(blocks, axis=0)


def spread(row, rows=8):
    return jnp.broadcast_to(row, (rows, row.shape[1]))


def pad_lanes(value, width=128):
    fill = jnp.zeros((value.shape[0], width - value.shape[1]), value.dtype)
    return jnp.concatenate([value, fill], axis=1)


def primitives(values):
    density = values[0]
    momentum = values[1:4]
    energy = values[4]
    inverse = 1.0 / density
    velocity = [m * inverse for m in momentum]
    kinetic = sum(m * v for m, v in zip(momentum, velocity))
    pressure = (GAMMA - 1.0) * (energy - 0.5 * kinetic)
    return (density, velocity, pressure, momentum, energy + pressure, inverse)


def along_flux(prims, normal):
    density, velocity, pressure, momentum, total, _ = prims
    along = sum(v * n for v, n in zip(velocity, normal))
    return (
        [density * along]
        + [m * along + pressure * n for m, n in zip(momentum, normal)]
        + [total * along]
    )


def along_flux_transposed(prims, cotangent):
    density, velocity, pressure, momentum, total, _ = prims
    scale = density * cotangent[0] + total * cotangent[4]
    for m in range(3):
        scale = scale + momentum[m] * cotangent[1 + m]
    return [velocity[i] * scale + pressure * cotangent[1 + i] for i in range(3)]


def cross(a, b):
    return [
        a[1] * b[2] - a[2] * b[1],
        a[2] * b[0] - a[0] * b[2],
        a[0] * b[1] - a[1] * b[0],
    ]


def added(a, b):
    return [x + y for x, y in zip(a, b)]


def signal_speed(prims, normal, area_square, area):
    density, velocity, pressure, _, _, inverse = prims
    along = sum(v * n for v, n in zip(velocity, normal))
    root = jnp.sqrt(along * along + SOFTENING * area_square)
    sound = jnp.sqrt(GAMMA * pressure * inverse)
    return root + sound * area, along, root, sound


def jump_of(inner, outer, normal, area_square, area):
    inner_prims = primitives(inner)
    outer_prims = primitives(outer)
    inner_speed = signal_speed(inner_prims, normal, area_square, area)[0]
    outer_speed = signal_speed(outer_prims, normal, area_square, area)[0]
    difference = inner_speed - outer_speed
    wave = 0.5 * (inner_speed + outer_speed) + 0.5 * jnp.sqrt(
        difference * difference + SOFTENING * area_square
    )
    inner_flux = along_flux(inner_prims, normal)
    outer_flux = along_flux(outer_prims, normal)
    return [
        0.5 * (outer_flux[v] - inner_flux[v]) - 0.5 * wave * (outer[v] - inner[v])
        for v in range(5)
    ]


def wave_gradient(inner_prims, outer_prims, normal, area_square, area):
    inner_speed, along_u, root_u, sound_u = signal_speed(inner_prims, normal, area_square, area)
    outer_speed, along_w, root_w, sound_w = signal_speed(outer_prims, normal, area_square, area)
    difference = inner_speed - outer_speed
    spread_root = jnp.sqrt(difference * difference + SOFTENING * area_square)
    over_u = 1.0 / root_u
    over_w = 1.0 / root_w
    over_area = 1.0 / area
    over_spread = 0.5 / spread_root
    result = []
    for i in range(3):
        slope_u = (along_u * inner_prims[1][i] + SOFTENING * normal[i]) * over_u + (
            sound_u * over_area
        ) * normal[i]
        slope_w = (along_w * outer_prims[1][i] + SOFTENING * normal[i]) * over_w + (
            sound_w * over_area
        ) * normal[i]
        result.append(
            0.5 * (slope_u + slope_w)
            + (difference * (slope_u - slope_w) + SOFTENING * normal[i]) * over_spread
        )
    return result


def pack_kernel(
    odd_ref, flow_ref, tangent_ref, places_ref, upper_ref, lower_ref, nodes_ref, a_ref, b_ref
):
    odd = odd_ref[0] == 1
    lane = lanes()
    group = lane // 32

    def faces(list_ref, row):
        index = pad_lanes(list_ref[...])
        index = spread(index)
        tiled = index
        for g in range(1, 4):
            tiled = jnp.where(group == g, pltpu.roll(index, 32 * g, 1), tiled)
        chunks = []
        for first in range(0, 12, 4):
            merged = None
            for g in range(4):
                v = first + g
                if v >= 10:
                    continue
                source = flow_ref if v < 5 else tangent_ref
                block = pad_lanes(source[v % 5, row : row + 16, :])
                block = pick(block, tiled)
                own = jnp.concatenate([group, group], axis=0) == g
                merged = jnp.where(own, block, 0.0 if merged is None else merged)
            chunks.append(merged)
        return jnp.concatenate(chunks, axis=0)

    up = faces(upper_ref, 48)
    down = faces(lower_ref, 0)
    node_index = spread(pad_lanes(nodes_ref[...]))
    places = jnp.concatenate([places_ref[...], jnp.zeros((5, 102), F32)], axis=0)
    nodes = pick(pad_lanes(places), node_index)
    none = jnp.zeros((8, 128), F32)
    up = jnp.concatenate([up, none], axis=0)
    down = jnp.concatenate([down, nodes], axis=0)
    a_ref[...] = jnp.where(odd, down, up)
    b_ref[...] = jnp.where(odd, up, down)


def face_pairs(ref, v):
    value = ref[v]
    sides = []
    for s in range(2):
        first = value[48 * s : 48 * s + 16]
        second = jnp.concatenate(
            [value[16 * i + 12 * s : 16 * i + 12 * s + 4] for i in range(4)], axis=0
        )
        third = ref[pl.ds(v, 1), pl.ds(3 * s, 16, stride=4), :][0]
        sides.append(jnp.concatenate([first, second, third], axis=0))
    return pair(sides[0], sides[1])


def volume_pairs(ref, v):
    return pair(ref[v, 0:32, :], ref[v, 32:64, :])


def corner_values(index, own_rows, halo_rows):
    local = index < 102
    own_index = jnp.where(local, index, 0)
    halo_index = jnp.where(local, 0, index - 102)
    result = []
    for i in range(3):
        own = pick(spread(own_rows[i : i + 1]), own_index)
        halo = pick(spread(halo_rows[i : i + 1]), halo_index)
        result.append(jnp.where(local, own, halo))
    return result


def corner_operand(values):
    low = lanes() < 64
    blocks = [
        jnp.concatenate([jnp.where(low, v, 0.0), jnp.where(low, 0.0, v)], axis=0) for v in values
    ]
    return jnp.concatenate(blocks, axis=1)


def columns(array, rows, i):
    return array[rows, 128 * i : 128 * i + 128]


def tangents_of(spans):
    volume = [[columns(spans, slice(32 * j, 32 * j + 32), i) for i in range(3)] for j in range(3)]
    faces = [
        [columns(spans, slice(96 + 48 * w, 144 + 48 * w), i) for i in range(3)] for w in range(2)
    ]
    return volume, faces


def folded(product, v):
    block = product[:, 128 * v : 128 * v + 128]
    return block[0:64] + pltpu.roll(block[64:128], 64, 1)


def side_sign():
    return jnp.where(lanes(48) < 64, -1.0, 1.0).astype(F32)


def main_kernel(
    odd_ref,
    far_ref,
    damping_ref,
    flow_ref,
    tangent_ref,
    places_ref,
    neighbour_ref,
    nodes_ref,
    sends_ref,
    flags_ref,
    a_ref,
    b_ref,
    assemble_ref,
    transposed_ref,
    corner_ref,
    corner_transposed_ref,
    residual_ref,
    change_ref,
    table_ref,
    send_a_ref,
    send_b_ref,
    spans_ref,
    outer_ref,
    slopes_ref,
    joined_ref,
):
    odd = odd_ref[0] == 1
    lane = lanes()
    low = lane < 64
    low16 = lanes(16) < 64
    from_a = a_ref[...]
    from_b = b_ref[...]
    lower = jnp.where(odd, from_a, from_b)
    upper = jnp.where(odd, from_b, from_a)

    node_index = pair(nodes_ref[...], nodes_ref[...])
    places = pad_lanes(places_ref[...])
    corners = corner_values(node_index, places, upper[48:56])
    relative = [c - c[0:1] for c in corners]
    spans = dot(corner_ref[...], corner_operand(relative))
    spans_ref[...] = spans
    volume_spans, face_spans = tangents_of(spans)
    normals = [cross(volume_spans[(j + 1) % 3], volume_spans[(j + 2) % 3]) for j in range(3)]
    sign = side_sign()
    face_normal = [sign * n for n in cross(face_spans[0], face_spans[1])]
    area_square = sum(n * n for n in face_normal)
    area = jnp.sqrt(area_square)

    inner = [face_pairs(flow_ref, v) for v in range(5)]
    inner_change = [face_pairs(tangent_ref, v) for v in range(5)]
    neighbours = neighbour_ref[...]
    listed = [
        spread(pair(neighbours[2 * j : 2 * j + 1], neighbours[2 * j + 1 : 2 * j + 2]))
        for j in range(3)
    ]
    gather_index = []
    for j in range(3):
        local = jnp.where(listed[j] < 64, listed[j], 0)
        gather_index.append(jnp.where(low, local + 64, local))
    slot = jnp.clip(listed[0] - 64, 0, 31)
    far16 = [jnp.concatenate([m, m], axis=0) == 96 for m in listed]
    halo16 = jnp.concatenate([listed[0], listed[0]], axis=0) >= 64

    def outside(face_values, v, far_value):
        rows = []
        for j in range(3):
            block = pick(face_values[16 * j : 16 * j + 16], gather_index[j])
            if j == 0:
                base, g = 16 * (v // 4), v % 4
                shifted_slot = slot + 32 * g
                below = pick(lower[base : base + 16], shifted_slot)
                above = pick(upper[base : base + 16], shifted_slot)
                block = jnp.where(halo16, jnp.where(low16, below, above), block)
            rows.append(jnp.where(far16[j], far_value, block))
        return jnp.concatenate(rows, axis=0)

    outer = [outside(inner[v], v, far_ref[v]) for v in range(5)]
    outer_change = [outside(inner_change[v], 5 + v, 0.0) for v in range(5)]
    for v in range(5):
        outer_ref[v] = outer[v]

    jump, jump_change = jax.jvp(
        lambda u, w: jump_of(u, w, face_normal, area_square, area),
        (inner, outer),
        (inner_change, outer_change),
    )
    state = [volume_pairs(flow_ref, v) for v in range(5)]
    state_change = [volume_pairs(tangent_ref, v) for v in range(5)]

    def volume_flux(u):
        prims = primitives(u)
        return [along_flux(prims, normals[j]) for j in range(3)]

    fluxes, flux_changes = jax.jvp(volume_flux, (state,), (state_change,))
    stacked = [
        jnp.concatenate([fluxes[0][v], fluxes[1][v], fluxes[2][v], jump[v]], axis=0)
        for v in range(5)
    ] + [
        jnp.concatenate(
            [flux_changes[0][v], flux_changes[1][v], flux_changes[2][v], jump_change[v]], axis=0
        )
        for v in range(5)
    ]
    assemble = assemble_ref[...]
    product = dot(assemble, jnp.concatenate(stacked, axis=1))
    residual = [folded(product, v) for v in range(5)]
    for v in range(5):
        residual_ref[v] = residual[v][:, 0:64]
        change_ref[v] = folded(product, 5 + v)[:, 0:64]

    weight = flags_ref[...].astype(F32)
    weight = pair(weight, weight)
    low64 = lanes(64) < 64
    seeds = []
    for v in range(5):
        seed = residual[v] * weight
        seeds.append(
            jnp.concatenate(
                [jnp.where(low64, seed, 0.0), jnp.where(low64, 0.0, pltpu.roll(seed, 64, 1))],
                axis=0,
            )
        )
    back = dot(transposed_ref[...], jnp.concatenate(seeds, axis=1))
    prims = primitives(state)
    normal_bar = []
    for j in range(3):
        cotangent = [columns(back, slice(32 * j, 32 * j + 32), v) for v in range(5)]
        normal_bar.append(along_flux_transposed(prims, cotangent))
    cotangent = [columns(back, slice(96, 144), v) for v in range(5)]
    inner_prims = primitives(inner)
    outer_prims = primitives(outer)
    slopes = wave_gradient(inner_prims, outer_prims, face_normal, area_square, area)
    for i in range(3):
        slopes_ref[i] = slopes[i]
    lift = sum(c * (w - u) for c, w, u in zip(cotangent, outer, inner))
    from_outer = along_flux_transposed(outer_prims, cotangent)
    from_inner = along_flux_transposed(inner_prims, cotangent)
    face_bar = [
        (0.5 * sign) * (from_outer[i] - from_inner[i] - lift * slopes[i]) for i in range(3)
    ]
    span_bar = []
    for j in range(3):
        first = cross(volume_spans[(j + 1) % 3], normal_bar[(j + 2) % 3])
        second = cross(normal_bar[(j + 1) % 3], volume_spans[(j + 2) % 3])
        span_bar.append(added(first, second))
    face_span_bar = [cross(face_spans[1], face_bar), cross(face_bar, face_spans[0])]
    stacked_bar = jnp.concatenate(
        [
            jnp.concatenate(
                [span_bar[j][i] for j in range(3)] + [face_span_bar[w][i] for w in range(2)],
                axis=0,
            )
            for i in range(3)
        ],
        axis=1,
    )
    corner_bar = dot(corner_transposed_ref[...], stacked_bar)
    smoothing = damping_ref[1]
    pieces = []
    for i in range(3):
        block = columns(corner_bar, slice(0, 16), i)
        bar = block[0:8] + pltpu.roll(block[8:16], 64, 1)
        bar = bar + smoothing * weight * columns(spans, slice(192, 200), i)
        pieces.append(bar)
    pieces.append(spread(weight))
    gradient = jnp.concatenate(pieces, axis=0)
    gradient = jnp.where(lanes(32) < 64, gradient, pltpu.roll(gradient, 64, 1))
    row_corner = lax.broadcasted_iota(jnp.int32, (32, 128), 0) % 8
    half = jnp.where(lanes(32) < 64, 0, 1)
    left = []
    right = []
    node_row = lax.broadcasted_iota(jnp.int32, (256, 128), 0)
    node_row = jnp.where(node_row < 128, node_row, node_row - 26)
    for p in range(4):
        left.append(jnp.where(row_corner == 2 * p + half, gradient, 0.0))
        named = jnp.where(low[0:1], node_index[2 * p : 2 * p + 1], node_index[2 * p + 1 : 2 * p + 2])
        right.append((node_row == named).astype(F32))
    right = [
        jnp.where((node_row[:, :] < 102) | (lax.broadcasted_iota(jnp.int32, (256, 128), 0) >= 128), r, 0.0)
        for r in right
    ]
    scattered = dot_transposed(jnp.concatenate(left, axis=1), jnp.concatenate(right, axis=1))
    rows = [jnp.sum(scattered[8 * i : 8 * i + 8], axis=0, keepdims=True) for i in range(4)]
    table = jnp.concatenate(rows + [jnp.zeros((4, 256), F32)], axis=0)
    table_ref[...] = table
    send_index = spread(pad_lanes(sends_ref[...]))
    up = table[:, 128:256]
    down = jnp.where(lane < 51, pick(table[:, 0:128], send_index), 0.0)
    send_a_ref[...] = jnp.where(odd, down, up)
    send_b_ref[...] = jnp.where(odd, up, down)
    joined_ref[...] = jnp.zeros((8, 128), F32)


def second_kernel(
    odd_ref,
    damping_ref,
    flow_ref,
    nodes_ref,
    sends_ref,
    flags_ref,
    table_ref,
    a_ref,
    b_ref,
    spans_ref,
    outer_ref,
    slopes_ref,
    assemble_ref,
    corner_ref,
    descent_ref,
    sums_ref,
):
    odd = odd_ref[0] == 1
    lane = lanes()
    from_a = a_ref[...]
    from_b = b_ref[...]
    lower = jnp.where(odd, from_a, from_b)
    upper = jnp.where(odd, from_b, from_a)
    table = table_ref[...]
    send_row = jnp.where(lane[0:1] < 51, pad_lanes(sends_ref[...]), -1)
    chosen = (lax.broadcasted_iota(jnp.int32, (128, 128), 0) == send_row).astype(F32)
    own = table[:, 0:128] + dot_transposed(jnp.where(lane < 51, lower, 0.0), chosen)
    halo = table[:, 128:256] + upper
    own = -jnp.where(own[3:4] > 0.5, own, 0.0)
    halo = -jnp.where(halo[3:4] > 0.5, halo, 0.0)
    descent_ref[...] = own[0:3]
    moved = jnp.where(lax.broadcasted_iota(jnp.int32, (8, 128), 0) < 3, own, 0.0)
    norm = jnp.sum(moved * moved, axis=(0, 1), keepdims=True)

    node_index = pair(nodes_ref[...], nodes_ref[...])
    steps = corner_values(node_index, own, halo)
    moves = dot(corner_ref[...], corner_operand(steps))
    volume_moves, face_moves = tangents_of(moves)
    volume_spans, face_spans = tangents_of(spans_ref[...])
    state = primitives([volume_pairs(flow_ref, v) for v in range(5)])
    fluxes = []
    for j in range(3):
        a, b = (j + 1) % 3, (j + 2) % 3
        normal_move = added(
            cross(volume_moves[a], volume_spans[b]), cross(volume_spans[a], volume_moves[b])
        )
        fluxes.append(along_flux(state, normal_move))
    sign = side_sign()
    face_move = [
        sign * n
        for n in added(cross(face_moves[0], face_spans[1]), cross(face_spans[0], face_moves[1]))
    ]
    inner = [face_pairs(flow_ref, v) for v in range(5)]
    outer = [outer_ref[v] for v in range(5)]
    inner_flux = along_flux(primitives(inner), face_move)
    outer_flux = along_flux(primitives(outer), face_move)
    wave_move = sum(slopes_ref[i] * face_move[i] for i in range(3))
    jump = [
        0.5 * (outer_flux[v] - inner_flux[v] - wave_move * (outer[v] - inner[v]))
        for v in range(5)
    ]
    stacked = [
        jnp.concatenate([fluxes[0][v], fluxes[1][v], fluxes[2][v], jump[v]], axis=0)
        for v in range(5)
    ]
    product = dot(assemble_ref[...], jnp.concatenate(stacked, axis=1))
    square = None
    for v in range(5):
        change = folded(product, v)
        square = change * change if square is None else square + change * change
    weight = flags_ref[...].astype(F32)
    weight = pad_lanes(weight)
    curvature = jnp.sum(jnp.sum(square, axis=0, keepdims=True) * weight, axis=1, keepdims=True)
    bend = sum(steps[i] * columns(moves, slice(192, 200), i) for i in range(3))
    bending = damping_ref[1] * jnp.sum(
        jnp.sum(bend, axis=0, keepdims=True) * weight, axis=1, keepdims=True
    )
    sums_ref[...] = jnp.where(
        lane[0:1] == 0, norm, jnp.where(lane[0:1] == 1, curvature + bending, 0.0)
    )


def call(kernel, out_shape, smem, arrays):
    scalar = pl.BlockSpec(memory_space=pltpu.SMEM)
    vector = pl.BlockSpec(memory_space=pltpu.VMEM)
    return pl.pallas_call(
        kernel,
        out_shape=[jax.ShapeDtypeStruct(s, F32) for s in out_shape],
        in_specs=[scalar] * smem + [vector] * (len(arrays) - smem),
        out_specs=[vector] * len(out_shape),
        name=kernel.__name__,
    )(*arrays)


def exchange(value_a, value_b, count):
    b = lax.ppermute(
        value_b,
        "parts",
        [(i, (i - 1) % count if i % 2 == 0 else (i + 1) % count) for i in range(count)],
    )
    a = lax.ppermute(value_a, "parts", [(i, i ^ 1) for i in range(count)])
    return a, b


def summed(row, count):
    inner = min(16, count)
    near = [[base + g for g in range(inner)] for base in range(0, count, inner)]
    far = [[base + inner * g for g in range(count // inner)] for base in range(inner)]
    for groups in (near, far):
        size = len(groups[0])
        if size > 1:
            sent = jnp.broadcast_to(row[None], (size,) + row.shape)
            row = jnp.sum(
                lax.all_to_all(sent, "parts", 0, 0, axis_index_groups=groups), axis=0
            )
    return row


def body(
    flow_state,
    state_tangent,
    far_field,
    coordinates,
    damping,
    face_neighbour,
    element_nodes,
    upper_sends,
    lower_sends,
    node_sends,
    shock_flags,
):
    count = lax.axis_size("parts")
    assemble, corner = constant_matrices()
    odd = (lax.axis_index("parts") % 2).astype(jnp.int32).reshape(1)
    sends_row = node_sends.reshape(1, 51)
    flags_row = shock_flags.reshape(1, 64)
    pack_a, pack_b = call(
        pack_kernel,
        [(56, 128)] * 2,
        1,
        (
            odd,
            flow_state,
            state_tangent,
            coordinates,
            upper_sends.reshape(1, 32),
            lower_sends.reshape(1, 32),
            sends_row,
        ),
    )
    got_a, got_b = exchange(pack_a, pack_b, count)
    residual, change, table, send_a, send_b, spans, outer, slopes, _ = call(
        main_kernel,
        [
            (5, 64, 64),
            (5, 64, 64),
            (8, 256),
            (8, 128),
            (8, 128),
            (200, 384),
            (5, 48, 128),
            (3, 48, 128),
            (8, 128),
        ],
        3,
        (
            odd,
            far_field,
            damping,
            flow_state,
            state_tangent,
            coordinates,
            face_neighbour,
            element_nodes,
            sends_row,
            flags_row,
            got_a,
            got_b,
            jnp.asarray(assemble),
            jnp.asarray(assemble.T.copy()),
            jnp.asarray(corner),
            jnp.asarray(corner[:192].T.copy()),
        ),
    )
    back_a, back_b = exchange(send_a, send_b, count)
    descent, sums = call(
        second_kernel,
        [(3, 128), (1, 128)],
        2,
        (
            odd,
            damping,
            flow_state,
            element_nodes,
            sends_row,
            flags_row,
            table,
            back_a,
            back_b,
            spans,
            outer,
            slopes,
            jnp.asarray(assemble),
            jnp.asarray(corner),
        ),
    )
    total = summed(sums[0], count)
    step = total[0] / (total[1] + damping[0] * total[0])
    return (residual, change, step * descent[:, 0:102])


def solution(mesh):
    in_specs = (
        P(None, None, "parts"),
        P(None, None, "parts"),
        P(),
        P(None, "parts"),
        P(),
        P(None, "parts"),
        P(None, "parts"),
        P("parts"),
        P("parts"),
        P("parts"),
        P("parts"),
    )
    out_specs = (P(None, None, "parts"), P(None, None, "parts"), P(None, "parts"))
    return jax.shard_map(body, mesh=mesh, in_specs=in_specs, out_specs=out_specs, check_vma=False)
```

profile of v0, /device:TPU:1, one launch (start us, length us, event | category | flops | bytes accessed | tf_op | source)
XLA Modules:
  0.0 76.1 jit_solution(1070957025150181114)
XLA Ops:
  0.6 1.8 %pack_kernel.1 = (f32[56,128]{1,0:T(8,128)}, f32[56,128]{1,0:T(8,128)}) custom-call(s32[1]{0:T(128)} %bitcast.odd_ref, f32[5,64,64]{2,1,0:T(8,128)} %flow_ref.5, f32[5,64,64]{2,1,0:T(8,128)} %tangent_ref.3, f32[3,102]{1,0:T(4,128)} %places_ref.3, s32[1,32]{1,0:T(1,128)} %bitcast.20, s32[1,32]{1,0:T(1,128)} %bitcast.21, s32[1,51]{1,0:T(1,128)} %bitcast.14), custom_call_target="tpu_custom_call" | custom-call | tf_op jit(solution)/shard_map/pack_kernel/pallas_call | solution.py:607
  2.5 8.7 %collective-permute-start = (f32[56,128]{1,0:T(8,128)}, f32[56,128]{1,0:T(8,128)S(1)}, u32[]{:S(2)}, u32[]{:S(2)}) collective-permute-start(f32[56,128]{1,0:T(8,128)} %get-tuple-element.15), channel_id=1, source_target_pairs={{0,1},{1,0},{2,3},{3,2},{4,5},{5,4},{6,7},{7,6},{8,9},{9,8},{10,11... | collective-permute-start | bytes 86024 | tf_op jit(solution)/shard_map/ppermute | solution.py:622
  11.2 1.9 %collective-permute-start.1 = (f32[56,128]{1,0:T(8,128)}, f32[56,128]{1,0:T(8,128)S(1)}, u32[]{:S(2)}, u32[]{:S(2)}) collective-permute-start(f32[56,128]{1,0:T(8,128)} %get-tuple-element.16), channel_id=1, source_target_pairs={{0,511},{1,2},{2,1},{3,4},{4,3},{5,6},{6,5},{7,8},{8,7},{9,10},{10... | collective-permute-start | bytes 86024 | tf_op jit(solution)/shard_map/ppermute | solution.py:617
  13.1 0.0 collective-permute-done.a_ref
  13.2 0.0 copy-start
  13.2 3.5 %collective-permute-done.1.b_ref = f32[56,128]{1,0:T(8,128)S(1)} collective-permute-done((f32[56,128]{1,0:T(8,128)}, f32[56,128]{1,0:T(8,128)S(1)}, u32[]{:S(2)}, u32[]{:S(2)}) %collective-permute-start.1) | collective-permute-done | bytes 28704 | tf_op jit(solution)/shard_map/ppermute | solution.py:617
  16.6 0.0 copy-done
  16.6 0.6 copy-done.1
  17.2 4.9 %main_kernel.1 = (f32[5,64,64]{2,1,0:T(8,128)}, f32[5,64,64]{2,1,0:T(8,128)}, f32[8,256]{1,0:T(8,128)}, f32[8,128]{1,0:T(8,128)}, f32[8,128]{1,0:T(8,128)}, /*in...) custom-call(s32[1]{0:T(128)} %bitcast.odd_ref, f32[5]{0:T(128)} %far_ref.1, ...), custom_call_target="tpu_custom_call" | custom-call | tf_op jit(solution)/shard_map/main_kernel/pallas_call | solution.py:607
  22.1 9.1 %collective-permute-start.2 = (f32[8,128]{1,0:T(8,128)}, f32[8,128]{1,0:T(8,128)S(1)}, u32[]{:S(2)}, u32[]{:S(2)}) collective-permute-start(f32[8,128]{1,0:T(8,128)} %get-tuple-element.20), channel_id=1, source_target_pairs={{0,1},{1,0},{2,3},{3,2},{4,5},{5,4},{6,7},{7,6},{8,9},{9,8},{10,11... | collective-permute-start | bytes 12296 | tf_op jit(solution)/shard_map/ppermute | solution.py:622
  31.2 1.9 %collective-permute-start.3 = (f32[8,128]{1,0:T(8,128)}, f32[8,128]{1,0:T(8,128)S(1)}, u32[]{:S(2)}, u32[]{:S(2)}) collective-permute-start(f32[8,128]{1,0:T(8,128)} %get-tuple-element.21), channel_id=1, source_target_pairs={{0,511},{1,2},{2,1},{3,4},{4,3},{5,6},{6,5},{7,8},{8,7},{9,10},{10... | collective-permute-start | bytes 12296 | tf_op jit(solution)/shard_map/ppermute | solution.py:617
  33.1 0.0 collective-permute-done.2.a_ref
  33.1 0.0 copy-start.2
  33.1 3.2 %collective-permute-done.3.b_ref = f32[8,128]{1,0:T(8,128)S(1)} collective-permute-done((f32[8,128]{1,0:T(8,128)}, f32[8,128]{1,0:T(8,128)S(1)}, u32[]{:S(2)}, u32[]{:S(2)}) %collective-permute-start.3) | collective-permute-done | bytes 4128 | tf_op jit(solution)/shard_map/ppermute | solution.py:617
  36.3 0.6 copy-done.3
  36.9 3.5 %second_kernel.1 = (f32[3,128]{1,0:T(4,128)}, f32[1,128]{1,0:T(1,128)}) custom-call(s32[1]{0:T(128)} %bitcast.odd_ref, f32[2]{0:T(128)} %damping_ref.3, f32[5,64,64]{2,1,0:T(8,128)} %flow_ref.5, s32[8,64]{1,0:T(8,128)} %nodes_ref.3, s32[1,51]{1,0:T(1,128)} %bitcast.16, s32[1,64]{1,0:T(1,128)} %bitcast.18, f32[8,256]{1,0:T(8,128)} %get-tuple-element.19.table_ref, ...), custom_call_target="tpu_custom_call" | custom-call | tf_op jit(solution)/shard_map/second_kernel/pallas_call | solution.py:607
  40.4 0.6 copy-done.6
  41.0 14.9 %all_to_all.12 = f32[16,1,128]{2,1,0:T(1,128)S(1)} all-to-all(f32[16,1,128]{2,1,0:T(1,128)S(1)} %broadcast_in_dim.4), channel_id=1, replica_groups={{0,1,2,3,4,5,6,7,8,9,10,11,12,13,14,15},{16,17,18,19,20,21,22,23,24,25,..., dimensions={0} | all-to-all | bytes 16384 | tf_op jit(solution)/shard_map/all_to_all | solution.py:635
  56.0 16.2 %all_to_all.13 = f32[32,1,128]{2,1,0:T(1,128)S(1)} all-to-all(f32[32,1,128]{2,1,0:T(1,128)S(1)} %broadcast_in_dim.5), channel_id=1, replica_groups={{0,16,32,48,64,80,96,112,128,144,160,176,192,208,224,240,256,272,288,30..., dimensions={0} | all-to-all | bytes 32768 | tf_op jit(solution)/shard_map/all_to_all | solution.py:635
  72.2 0.6 fusion
  72.9 0.7 copy-done.4
  74.8 0.0 copy-start.5
  75.5 0.0 copy-done.5
  75.5 0.6 slice_multiply_fusion
  (9 shorter events, 0.1 us)
Async XLA Ops:
  2.5 10.7 %collective-permute-start = (f32[56,128]{1,0:T(8,128)}, f32[56,128]{1,0:T(8,128)S(1)}, u32[]{:S(2)}, u32[]{:S(2)}) collective-permute-start(f32[56,128]{1,0:T(8,128)} %get-tuple-element.15), channel_id=1, source_target_pairs={{0,1},{1,0},{2,3},{3,2},{4,5},{5,4},{6,7},{7,6},{8,9},{9,8},{10,11... | collective-permute-start | bytes 86024 | tf_op jit(solution)/shard_map/ppermute | solution.py:622
  11.2 5.4 %collective-permute-start.1 = (f32[56,128]{1,0:T(8,128)}, f32[56,128]{1,0:T(8,128)S(1)}, u32[]{:S(2)}, u32[]{:S(2)}) collective-permute-start(f32[56,128]{1,0:T(8,128)} %get-tuple-element.16), channel_id=1, source_target_pairs={{0,511},{1,2},{2,1},{3,4},{4,3},{5,6},{6,5},{7,8},{8,7},{9,10},{10... | collective-permute-start | bytes 86024 | tf_op jit(solution)/shard_map/ppermute | solution.py:617
  13.2 3.5 %copy-start = (f32[56,128]{1,0:T(8,128)}, f32[56,128]{1,0:T(8,128)S(1)}, u32[]{:S(2)}) copy-start(f32[56,128]{1,0:T(8,128)S(1)} %collective-permute-done.a_ref) | copy-start | bytes 86020
  16.6 0.6 copy-start.1
  22.1 11.0 %collective-permute-start.2 = (f32[8,128]{1,0:T(8,128)}, f32[8,128]{1,0:T(8,128)S(1)}, u32[]{:S(2)}, u32[]{:S(2)}) collective-permute-start(f32[8,128]{1,0:T(8,128)} %get-tuple-element.20), channel_id=1, source_target_pairs={{0,1},{1,0},{2,3},{3,2},{4,5},{5,4},{6,7},{7,6},{8,9},{9,8},{10,11... | collective-permute-start | bytes 12296 | tf_op jit(solution)/shard_map/ppermute | solution.py:622
  31.2 5.1 %collective-permute-start.3 = (f32[8,128]{1,0:T(8,128)}, f32[8,128]{1,0:T(8,128)S(1)}, u32[]{:S(2)}, u32[]{:S(2)}) collective-permute-start(f32[8,128]{1,0:T(8,128)} %get-tuple-element.21), channel_id=1, source_target_pairs={{0,511},{1,2},{2,1},{3,4},{4,3},{5,6},{6,5},{7,8},{8,7},{9,10},{10... | collective-permute-start | bytes 12296 | tf_op jit(solution)/shard_map/ppermute | solution.py:617
  33.1 3.2 %copy-start.2 = (f32[8,128]{1,0:T(8,128)}, f32[8,128]{1,0:T(8,128)S(1)}, u32[]{:S(2)}) copy-start(f32[8,128]{1,0:T(8,128)S(1)} %collective-permute-done.2.a_ref) | copy-start | bytes 12292
  36.3 0.6 copy-start.3
  40.4 0.6 copy-start.6
  72.9 0.7 copy-start.4
  74.8 0.7 copy-start.5
where the time goes:
time: 76.5 us; the launch traced here: 76.1 us
  blocking collectives  31.1 us (41%)
  starting transfers between devices  21.7 us (28%)
  Pallas kernels  10.2 us (13%)
  waiting for transfers between devices  6.64 us (9%)
  local copies, waits for them, and re-layouts  3.17 us (4%)
  between operations  2.68 us (4%)
    all_to_all x2, blocking collectives, summed(): lax.all_to_all(sent, 'parts', 0, 0, axis_index_groups=groups)  31.1 us
    ppermute x2, starting transfers between devices, exchange(): a = lax.ppermute(value_a, 'parts', [(i, i ^ 1) for i in range(count)])  17.8 us
    pallas_call x3, Pallas kernels, call(): pl.pallas_call(kernel, out_shape=[jax.ShapeDtypeStruct(s, F32) for s in o...  10.2 us
    ppermute x2, waiting for transfers between devices, exchange(): lax.ppermute(value_b, 'parts', [(i, (i - 1) % count if i % 2 == 0 else (i...  6.64 us
    ppermute x2, starting transfers between devices, exchange(): lax.ppermute(value_b, 'parts', [(i, (i - 1) % count if i % 2 == 0 else (i...  3.84 us
    unnamed x14, local copies, waits for them, and re-layouts  2.51 us
  transfers between devices with their start and end apart: 4, of which 2 were waited for; matrix products, arithmetic and copies ran while one was open for 0% of the time, Pallas kernels for 0%

commit v1 on v0

--- a/solution.py
+++ b/solution.py
@@ -1,4 +1,3 @@
-import functools
 import math
 
 import jax
@@ -8,6 +7,7 @@
 from jax.experimental import pallas as pl
 from jax.experimental.pallas import tpu as pltpu
 from jax.sharding import PartitionSpec as P
+
 
 GAMMA = 1.4
 SOFTENING = 0.01
@@ -69,7 +69,7 @@
 
 
 def constant_matrices():
-    points, weights, derivative = lobatto_tables()
+    _, weights, derivative = lobatto_tables()
     volume = np.einsum("a,b,c->abc", weights, weights, weights).reshape(64)
     face = np.einsum("a,b->ab", weights, weights).reshape(16)
     eye = np.eye(4)
@@ -101,14 +101,34 @@
     return assemble.astype(np.float32), corner.astype(np.float32)
 
 
+def constant_tables():
+    assemble, corner = constant_matrices()
+    tables = np.zeros((488, 256), np.float32)
+    tables[0:128, 0:144] = assemble
+    tables[128:272, 0:128] = assemble.T
+    tables[272:472, 0:16] = corner
+    tables[472:488, 0:192] = corner[0:192].T
+    return tables
+
+
 def dot(a, b):
     return jnp.dot(a, b, precision=HIGHEST, preferred_element_type=F32)
 
 
-def dot_transposed(a, b):
-    return lax.dot_general(
-        a, b, (((1,), (1,)), ((), ())), precision=HIGHEST, preferred_element_type=F32
-    )
+def placed(a, chosen):
+    rows = a.shape[0]
+    parts = []
+    for _ in range(3):
+        part = a.astype(jnp.bfloat16)
+        parts.append(part)
+        a = a - part.astype(F32)
+    product = lax.dot_general(
+        jnp.concatenate(parts, axis=0),
+        chosen,
+        (((1,), (1,)), ((), ())),
+        preferred_element_type=F32,
+    )
+    return product[0:rows] + product[rows : 2 * rows] + product[2 * rows : 3 * rows]
 
 
 def lanes(rows=8):
@@ -178,7 +198,7 @@
 
 
 def signal_speed(prims, normal, area_square, area):
-    density, velocity, pressure, _, _, inverse = prims
+    _, velocity, pressure, _, _, inverse = prims
     along = sum(v * n for v, n in zip(velocity, normal))
     root = jnp.sqrt(along * along + SOFTENING * area_square)
     sound = jnp.sqrt(GAMMA * pressure * inverse)
@@ -226,10 +246,46 @@
     return result
 
 
+def on_odd():
+    return (lax.axis_index("parts") & 1) == 1
+
+
 def pack_kernel(
-    odd_ref, flow_ref, tangent_ref, places_ref, upper_ref, lower_ref, nodes_ref, a_ref, b_ref
+    flow_hbm,
+    tangent_hbm,
+    places_hbm,
+    upper_hbm,
+    lower_hbm,
+    nodes_hbm,
+    a_ref,
+    b_ref,
+    flow_ref,
+    tangent_ref,
+    places_ref,
+    upper_ref,
+    lower_ref,
+    nodes_ref,
+    semaphores,
 ):
-    odd = odd_ref[0] == 1
+    copies = [
+        (flow_hbm.at[:, 0:16, :], flow_ref.at[:, 0:16, :]),
+        (flow_hbm.at[:, 48:64, :], flow_ref.at[:, 16:32, :]),
+        (tangent_hbm.at[:, 0:16, :], tangent_ref.at[:, 0:16, :]),
+        (tangent_hbm.at[:, 48:64, :], tangent_ref.at[:, 16:32, :]),
+        (places_hbm, places_ref),
+        (upper_hbm, upper_ref),
+        (lower_hbm, lower_ref),
+        (nodes_hbm, nodes_ref),
+    ]
+    copies = [
+        pltpu.make_async_copy(source, target, semaphores.at[i])
+        for i, (source, target) in enumerate(copies)
+    ]
+    for copy in copies:
+        copy.start()
+    for copy in copies:
+        copy.wait()
+    odd = on_odd()
     lane = lanes()
     group = lane // 32
 
@@ -254,7 +310,7 @@
             chunks.append(merged)
         return jnp.concatenate(chunks, axis=0)
 
-    up = faces(upper_ref, 48)
+    up = faces(upper_ref, 16)
     down = faces(lower_ref, 0)
     node_index = spread(pad_lanes(nodes_ref[...]))
     places = jnp.concatenate([places_ref[...], jnp.zeros((5, 102), F32)], axis=0)
@@ -324,17 +380,174 @@
     return jnp.where(lanes(48) < 64, -1.0, 1.0).astype(F32)
 
 
-def main_kernel(
-    odd_ref,
-    far_ref,
-    damping_ref,
+def ready_kernel(
     flow_ref,
     tangent_ref,
+    far_ref,
     places_ref,
     neighbour_ref,
     nodes_ref,
     sends_ref,
     flags_ref,
+    damping_ref,
+    tables_ref,
+    inner_ref,
+    state_ref,
+    outer_ref,
+    places_out,
+    border_ref,
+    node_index_ref,
+    send_index_ref,
+    named_ref,
+    chosen_ref,
+    weight_ref,
+    smoothing_ref,
+    assemble_ref,
+    transposed_ref,
+    corner_ref,
+    corner_transposed_ref,
+):
+    lane = lanes()
+    low = lane < 64
+    neighbours = neighbour_ref[...]
+    listed = [
+        spread(pair(neighbours[2 * j : 2 * j + 1], neighbours[2 * j + 1 : 2 * j + 2]))
+        for j in range(3)
+    ]
+    border_ref[...] = listed[0]
+    local = []
+    for j in range(3):
+        index = jnp.where(listed[j] < 64, listed[j], 0)
+        local.append(jnp.where(low, index + 64, index))
+    far = [jnp.concatenate([m, m], axis=0) == 96 for m in listed]
+    for v in range(10):
+        source = flow_ref if v < 5 else tangent_ref
+        inner = face_pairs(source, v % 5)
+        inner_ref[v] = inner
+        state_ref[v] = volume_pairs(source, v % 5)
+        far_value = far_ref[0:1, v : v + 1] if v < 5 else 0.0
+        for j in range(3):
+            rows = slice(16 * j, 16 * j + 16)
+            outer_ref[v, rows, :] = jnp.where(far[j], far_value, pick(inner[rows], local[j]))
+    places_out[...] = jnp.concatenate([pad_lanes(places_ref[...]), jnp.zeros((5, 128), F32)], axis=0)
+    node_index = pair(nodes_ref[...], nodes_ref[...])
+    node_index_ref[...] = node_index
+    send_row = pad_lanes(sends_ref[...])
+    send_index_ref[...] = spread(send_row)
+    table_row = lax.broadcasted_iota(jnp.int32, (256, 128), 0)
+    node_of_row = jnp.where(
+        table_row < 102, table_row, jnp.where(table_row < 128, -1, table_row - 26)
+    )
+    for p in range(4):
+        named = jnp.where(
+            low[0:1], node_index[2 * p : 2 * p + 1], node_index[2 * p + 1 : 2 * p + 2]
+        )
+        named_ref[:, 128 * p : 128 * p + 128] = (
+            (node_of_row == named).astype(F32).astype(jnp.bfloat16)
+        )
+    sent = jnp.where(lane[0:1] < 51, send_row, -1)
+    chosen_ref[...] = (
+        (lax.broadcasted_iota(jnp.int32, (128, 128), 0) == sent).astype(F32).astype(jnp.bfloat16)
+    )
+    weight = flags_ref[...].astype(F32)
+    weight_ref[...] = spread(pair(weight, weight))
+    smoothing_ref[...] = jnp.where(
+        lane == 0, damping_ref[0:1, 0:1], jnp.broadcast_to(damping_ref[0:1, 1:2], (8, 128))
+    )
+    assemble_ref[...] = tables_ref[0:128, 0:144]
+    transposed_ref[...] = tables_ref[128:272, 0:128]
+    corner_ref[...] = tables_ref[272:472, 0:16]
+    corner_transposed_ref[...] = tables_ref[472:488, 0:192]
+
+
+class Border:
+    def __init__(self, border, lower, upper):
+        self.slot = jnp.clip(border - 64, 0, 31)
+        halo = (border >= 64) & (border < 96)
+        low = lanes() < 64
+        self.below = jnp.concatenate([halo & low, halo & low], axis=0)
+        self.above = jnp.concatenate([halo & ~low, halo & ~low], axis=0)
+        self.lower = lower
+        self.upper = upper
+
+    def values(self, local, v):
+        rows = slice(16 * (v // 4), 16 * (v // 4) + 16)
+        slot = self.slot + 32 * (v % 4)
+        first = jnp.where(self.below, pick(self.lower[rows], slot), local[0:16])
+        first = jnp.where(self.above, pick(self.upper[rows], slot), first)
+        return jnp.concatenate([first, local[16:48]], axis=0)
+
+
+def geometry(volume_spans, face_spans):
+    normals = [cross(volume_spans[(j + 1) % 3], volume_spans[(j + 2) % 3]) for j in range(3)]
+    sign = side_sign()
+    face_normal = [sign * n for n in cross(face_spans[0], face_spans[1])]
+    area_square = sum(n * n for n in face_normal)
+    return normals, face_normal, area_square, jnp.sqrt(area_square)
+
+
+def volume_flux(state, normals):
+    prims = primitives(state)
+    return [along_flux(prims, normals[j]) for j in range(3)]
+
+
+def assembled(assemble, fluxes, jump):
+    stacked = [
+        jnp.concatenate([fluxes[0][v], fluxes[1][v], fluxes[2][v], jump[v]], axis=0)
+        for v in range(5)
+    ]
+    product = dot(assemble, jnp.concatenate(stacked, axis=1))
+    return [folded(product, v) for v in range(5)]
+
+
+def change_kernel(
+    inner_ref,
+    state_ref,
+    local_ref,
+    border_ref,
+    a_ref,
+    b_ref,
+    assemble_ref,
+    spans_ref,
+    outer_ref,
+    change_ref,
+    token_ref,
+):
+    odd = on_odd()
+    from_a = a_ref[...]
+    from_b = b_ref[...]
+    border = Border(border_ref[...], jnp.where(odd, from_a, from_b), jnp.where(odd, from_b, from_a))
+    volume_spans, face_spans = tangents_of(spans_ref[...])
+    normals, face_normal, area_square, area = geometry(volume_spans, face_spans)
+    inner = [inner_ref[v] for v in range(5)]
+    inner_change = [inner_ref[5 + v] for v in range(5)]
+    outer = [outer_ref[v] for v in range(5)]
+    outer_change = [border.values(local_ref[5 + v], 5 + v) for v in range(5)]
+    _, jump_change = jax.jvp(
+        lambda u, w: jump_of(u, w, face_normal, area_square, area),
+        (inner, outer),
+        (inner_change, outer_change),
+    )
+    state = [state_ref[v] for v in range(5)]
+    state_change = [state_ref[5 + v] for v in range(5)]
+    _, flux_changes = jax.jvp(lambda u: volume_flux(u, normals), (state,), (state_change,))
+    change = assembled(assemble_ref[...], flux_changes, jump_change)
+    for v in range(5):
+        change_ref[v] = change[v][:, 0:64]
+    token_ref[...] = jnp.zeros((8, 128), F32)
+
+
+def main_kernel(
+    inner_ref,
+    state_ref,
+    local_ref,
+    places_ref,
+    border_ref,
+    node_index_ref,
+    send_index_ref,
+    named_ref,
+    weight_ref,
+    smoothing_ref,
     a_ref,
     b_ref,
     assemble_ref,
@@ -342,101 +555,40 @@
     corner_ref,
     corner_transposed_ref,
     residual_ref,
-    change_ref,
     table_ref,
     send_a_ref,
     send_b_ref,
     spans_ref,
     outer_ref,
     slopes_ref,
-    joined_ref,
 ):
-    odd = odd_ref[0] == 1
+    odd = on_odd()
     lane = lanes()
-    low = lane < 64
-    low16 = lanes(16) < 64
     from_a = a_ref[...]
     from_b = b_ref[...]
     lower = jnp.where(odd, from_a, from_b)
     upper = jnp.where(odd, from_b, from_a)
 
-    node_index = pair(nodes_ref[...], nodes_ref[...])
-    places = pad_lanes(places_ref[...])
-    corners = corner_values(node_index, places, upper[48:56])
+    corners = corner_values(node_index_ref[...], places_ref[...], upper[48:56])
     relative = [c - c[0:1] for c in corners]
     spans = dot(corner_ref[...], corner_operand(relative))
     spans_ref[...] = spans
     volume_spans, face_spans = tangents_of(spans)
-    normals = [cross(volume_spans[(j + 1) % 3], volume_spans[(j + 2) % 3]) for j in range(3)]
+    normals, face_normal, area_square, area = geometry(volume_spans, face_spans)
     sign = side_sign()
-    face_normal = [sign * n for n in cross(face_spans[0], face_spans[1])]
-    area_square = sum(n * n for n in face_normal)
-    area = jnp.sqrt(area_square)
-
-    inner = [face_pairs(flow_ref, v) for v in range(5)]
-    inner_change = [face_pairs(tangent_ref, v) for v in range(5)]
-    neighbours = neighbour_ref[...]
-    listed = [
-        spread(pair(neighbours[2 * j : 2 * j + 1], neighbours[2 * j + 1 : 2 * j + 2]))
-        for j in range(3)
-    ]
-    gather_index = []
-    for j in range(3):
-        local = jnp.where(listed[j] < 64, listed[j], 0)
-        gather_index.append(jnp.where(low, local + 64, local))
-    slot = jnp.clip(listed[0] - 64, 0, 31)
-    far16 = [jnp.concatenate([m, m], axis=0) == 96 for m in listed]
-    halo16 = jnp.concatenate([listed[0], listed[0]], axis=0) >= 64
-
-    def outside(face_values, v, far_value):
-        rows = []
-        for j in range(3):
-            block = pick(face_values[16 * j : 16 * j + 16], gather_index[j])
-            if j == 0:
-                base, g = 16 * (v // 4), v % 4
-                shifted_slot = slot + 32 * g
-                below = pick(lower[base : base + 16], shifted_slot)
-                above = pick(upper[base : base + 16], shifted_slot)
-                block = jnp.where(halo16, jnp.where(low16, below, above), block)
-            rows.append(jnp.where(far16[j], far_value, block))
-        return jnp.concatenate(rows, axis=0)
-
-    outer = [outside(inner[v], v, far_ref[v]) for v in range(5)]
-    outer_change = [outside(inner_change[v], 5 + v, 0.0) for v in range(5)]
+
+    inner = [inner_ref[v] for v in range(5)]
+    border = Border(border_ref[...], lower, upper)
+    outer = [border.values(local_ref[v], v) for v in range(5)]
     for v in range(5):
         outer_ref[v] = outer[v]
-
-    jump, jump_change = jax.jvp(
-        lambda u, w: jump_of(u, w, face_normal, area_square, area),
-        (inner, outer),
-        (inner_change, outer_change),
-    )
-    state = [volume_pairs(flow_ref, v) for v in range(5)]
-    state_change = [volume_pairs(tangent_ref, v) for v in range(5)]
-
-    def volume_flux(u):
-        prims = primitives(u)
-        return [along_flux(prims, normals[j]) for j in range(3)]
-
-    fluxes, flux_changes = jax.jvp(volume_flux, (state,), (state_change,))
-    stacked = [
-        jnp.concatenate([fluxes[0][v], fluxes[1][v], fluxes[2][v], jump[v]], axis=0)
-        for v in range(5)
-    ] + [
-        jnp.concatenate(
-            [flux_changes[0][v], flux_changes[1][v], flux_changes[2][v], jump_change[v]], axis=0
-        )
-        for v in range(5)
-    ]
-    assemble = assemble_ref[...]
-    product = dot(assemble, jnp.concatenate(stacked, axis=1))
-    residual = [folded(product, v) for v in range(5)]
+    jump = jump_of(inner, outer, face_normal, area_square, area)
+    state = [state_ref[v] for v in range(5)]
+    residual = assembled(assemble_ref[...], volume_flux(state, normals), jump)
     for v in range(5):
         residual_ref[v] = residual[v][:, 0:64]
-        change_ref[v] = folded(product, 5 + v)[:, 0:64]
-
-    weight = flags_ref[...].astype(F32)
-    weight = pair(weight, weight)
+
+    weight = weight_ref[0:1]
     low64 = lanes(64) < 64
     seeds = []
     for v in range(5):
@@ -482,7 +634,7 @@
         axis=1,
     )
     corner_bar = dot(corner_transposed_ref[...], stacked_bar)
-    smoothing = damping_ref[1]
+    smoothing = smoothing_ref[0:1, 1:2]
     pieces = []
     for i in range(3):
         block = columns(corner_bar, slice(0, 16), i)
@@ -494,37 +646,24 @@
     gradient = jnp.where(lanes(32) < 64, gradient, pltpu.roll(gradient, 64, 1))
     row_corner = lax.broadcasted_iota(jnp.int32, (32, 128), 0) % 8
     half = jnp.where(lanes(32) < 64, 0, 1)
-    left = []
-    right = []
-    node_row = lax.broadcasted_iota(jnp.int32, (256, 128), 0)
-    node_row = jnp.where(node_row < 128, node_row, node_row - 26)
-    for p in range(4):
-        left.append(jnp.where(row_corner == 2 * p + half, gradient, 0.0))
-        named = jnp.where(low[0:1], node_index[2 * p : 2 * p + 1], node_index[2 * p + 1 : 2 * p + 2])
-        right.append((node_row == named).astype(F32))
-    right = [
-        jnp.where((node_row[:, :] < 102) | (lax.broadcasted_iota(jnp.int32, (256, 128), 0) >= 128), r, 0.0)
-        for r in right
-    ]
-    scattered = dot_transposed(jnp.concatenate(left, axis=1), jnp.concatenate(right, axis=1))
+    left = [jnp.where(row_corner == 2 * p + half, gradient, 0.0) for p in range(4)]
+    scattered = placed(jnp.concatenate(left, axis=1), named_ref[...])
     rows = [jnp.sum(scattered[8 * i : 8 * i + 8], axis=0, keepdims=True) for i in range(4)]
     table = jnp.concatenate(rows + [jnp.zeros((4, 256), F32)], axis=0)
     table_ref[...] = table
-    send_index = spread(pad_lanes(sends_ref[...]))
     up = table[:, 128:256]
-    down = jnp.where(lane < 51, pick(table[:, 0:128], send_index), 0.0)
+    down = jnp.where(lane < 51, pick(table[:, 0:128], send_index_ref[...]), 0.0)
     send_a_ref[...] = jnp.where(odd, down, up)
     send_b_ref[...] = jnp.where(odd, up, down)
-    joined_ref[...] = jnp.zeros((8, 128), F32)
 
 
 def second_kernel(
-    odd_ref,
-    damping_ref,
-    flow_ref,
-    nodes_ref,
-    sends_ref,
-    flags_ref,
+    inner_ref,
+    state_ref,
+    node_index_ref,
+    chosen_ref,
+    weight_ref,
+    smoothing_ref,
     table_ref,
     a_ref,
     b_ref,
@@ -533,19 +672,19 @@
     slopes_ref,
     assemble_ref,
     corner_ref,
+    _,
     descent_ref,
     sums_ref,
 ):
-    odd = odd_ref[0] == 1
+    odd = on_odd()
     lane = lanes()
     from_a = a_ref[...]
     from_b = b_ref[...]
     lower = jnp.where(odd, from_a, from_b)
     upper = jnp.where(odd, from_b, from_a)
     table = table_ref[...]
-    send_row = jnp.where(lane[0:1] < 51, pad_lanes(sends_ref[...]), -1)
-    chosen = (lax.broadcasted_iota(jnp.int32, (128, 128), 0) == send_row).astype(F32)
-    own = table[:, 0:128] + dot_transposed(jnp.where(lane < 51, lower, 0.0), chosen)
+    sixteen = jnp.concatenate([jnp.where(lane < 51, lower, 0.0), jnp.zeros((8, 128), F32)], axis=0)
+    own = table[:, 0:128] + placed(sixteen, chosen_ref[...])[0:8]
     halo = table[:, 128:256] + upper
     own = -jnp.where(own[3:4] > 0.5, own, 0.0)
     halo = -jnp.where(halo[3:4] > 0.5, halo, 0.0)
@@ -553,12 +692,11 @@
     moved = jnp.where(lax.broadcasted_iota(jnp.int32, (8, 128), 0) < 3, own, 0.0)
     norm = jnp.sum(moved * moved, axis=(0, 1), keepdims=True)
 
-    node_index = pair(nodes_ref[...], nodes_ref[...])
-    steps = corner_values(node_index, own, halo)
+    steps = corner_values(node_index_ref[...], own, halo)
     moves = dot(corner_ref[...], corner_operand(steps))
     volume_moves, face_moves = tangents_of(moves)
     volume_spans, face_spans = tangents_of(spans_ref[...])
-    state = primitives([volume_pairs(flow_ref, v) for v in range(5)])
+    state = primitives([state_ref[v] for v in range(5)])
     fluxes = []
     for j in range(3):
         a, b = (j + 1) % 3, (j + 2) % 3
@@ -571,7 +709,7 @@
         sign * n
         for n in added(cross(face_moves[0], face_spans[1]), cross(face_spans[0], face_moves[1]))
     ]
-    inner = [face_pairs(flow_ref, v) for v in range(5)]
+    inner = [inner_ref[v] for v in range(5)]
     outer = [outer_ref[v] for v in range(5)]
     inner_flux = along_flux(primitives(inner), face_move)
     outer_flux = along_flux(primitives(outer), face_move)
@@ -580,36 +718,40 @@
         0.5 * (outer_flux[v] - inner_flux[v] - wave_move * (outer[v] - inner[v]))
         for v in range(5)
     ]
-    stacked = [
-        jnp.concatenate([fluxes[0][v], fluxes[1][v], fluxes[2][v], jump[v]], axis=0)
-        for v in range(5)
-    ]
-    product = dot(assemble_ref[...], jnp.concatenate(stacked, axis=1))
-    square = None
-    for v in range(5):
-        change = folded(product, v)
-        square = change * change if square is None else square + change * change
-    weight = flags_ref[...].astype(F32)
-    weight = pad_lanes(weight)
+    square = sum(
+        change * change for change in assembled(assemble_ref[...], fluxes, jump)
+    )
+    weight = jnp.where(lane[0:1] < 64, weight_ref[0:1], 0.0)
     curvature = jnp.sum(jnp.sum(square, axis=0, keepdims=True) * weight, axis=1, keepdims=True)
     bend = sum(steps[i] * columns(moves, slice(192, 200), i) for i in range(3))
-    bending = damping_ref[1] * jnp.sum(
+    bending = smoothing_ref[0:1, 1:2] * jnp.sum(
         jnp.sum(bend, axis=0, keepdims=True) * weight, axis=1, keepdims=True
     )
-    sums_ref[...] = jnp.where(
-        lane[0:1] == 0, norm, jnp.where(lane[0:1] == 1, curvature + bending, 0.0)
-    )
-
-
-def call(kernel, out_shape, smem, arrays):
-    scalar = pl.BlockSpec(memory_space=pltpu.SMEM)
+    lower_sum = curvature + bending + smoothing_ref[0:1, 0:1] * norm
+    sums = jnp.where(lane[0:1] == 0, norm, jnp.where(lane[0:1] == 1, lower_sum, 0.0))
+    for i in range(sums_ref.shape[0]):
+        sums_ref[i] = sums
+
+
+def finish_kernel(sums_ref, descent_ref, update_ref):
+    total = jnp.sum(sums_ref[...], axis=0)
+    step = total[:, 0:1] / total[:, 1:2]
+    update_ref[...] = step * descent_ref[:, 0:102]
+
+
+def call(kernel, out_shape, arrays, cost=None, place=pltpu.VMEM, scratch=(), limit=16 << 20):
     vector = pl.BlockSpec(memory_space=pltpu.VMEM)
     return pl.pallas_call(
         kernel,
-        out_shape=[jax.ShapeDtypeStruct(s, F32) for s in out_shape],
-        in_specs=[scalar] * smem + [vector] * (len(arrays) - smem),
+        out_shape=[
+            s if isinstance(s, jax.ShapeDtypeStruct) else jax.ShapeDtypeStruct(s, F32)
+            for s in out_shape
+        ],
+        in_specs=[pl.BlockSpec(memory_space=place)] * len(arrays),
         out_specs=[vector] * len(out_shape),
-        name=kernel.__name__,
+        scratch_shapes=list(scratch),
+        compiler_params=pltpu.CompilerParams(vmem_limit_bytes=limit),
+        cost_estimate=cost,
     )(*arrays)
 
 
@@ -623,21 +765,7 @@
     return a, b
 
 
-def summed(row, count):
-    inner = min(16, count)
-    near = [[base + g for g in range(inner)] for base in range(0, count, inner)]
-    far = [[base + inner * g for g in range(count // inner)] for base in range(inner)]
-    for groups in (near, far):
-        size = len(groups[0])
-        if size > 1:
-            sent = jnp.broadcast_to(row[None], (size,) + row.shape)
-            row = jnp.sum(
-                lax.all_to_all(sent, "parts", 0, 0, axis_index_groups=groups), axis=0
-            )
-    return row
-
-
-def body(
+def step(
     flow_state,
     state_tangent,
     far_field,
@@ -651,16 +779,14 @@
     shock_flags,
 ):
     count = lax.axis_size("parts")
-    assemble, corner = constant_matrices()
-    odd = (lax.axis_index("parts") % 2).astype(jnp.int32).reshape(1)
     sends_row = node_sends.reshape(1, 51)
     flags_row = shock_flags.reshape(1, 64)
+    damping_row = damping.reshape(1, 2)
+    integer = jnp.int32
     pack_a, pack_b = call(
         pack_kernel,
         [(56, 128)] * 2,
-        1,
         (
-            odd,
             flow_state,
             state_tangent,
             coordinates,
@@ -668,12 +794,71 @@
             lower_sends.reshape(1, 32),
             sends_row,
         ),
+        place=pltpu.HBM,
+        limit=60 * 1024 * 1024,
+        scratch=(
+            pltpu.VMEM((5, 32, 64), F32),
+            pltpu.VMEM((5, 32, 64), F32),
+            pltpu.VMEM((3, 102), F32),
+            pltpu.VMEM((1, 32), integer),
+            pltpu.VMEM((1, 32), integer),
+            pltpu.VMEM((1, 51), integer),
+            pltpu.SemaphoreType.DMA((8,)),
+        ),
     )
     got_a, got_b = exchange(pack_a, pack_b, count)
-    residual, change, table, send_a, send_b, spans, outer, slopes, _ = call(
+    (
+        inner,
+        state,
+        local,
+        places,
+        border,
+        node_index,
+        send_index,
+        named,
+        chosen,
+        weight,
+        smoothing,
+        assemble,
+        transposed,
+        corner,
+        corner_transposed,
+    ) = call(
+        ready_kernel,
+        [
+            (10, 48, 128),
+            (10, 32, 128),
+            (10, 48, 128),
+            (8, 128),
+            jax.ShapeDtypeStruct((8, 128), integer),
+            jax.ShapeDtypeStruct((8, 128), integer),
+            jax.ShapeDtypeStruct((8, 128), integer),
+            jax.ShapeDtypeStruct((256, 512), jnp.bfloat16),
+            jax.ShapeDtypeStruct((128, 128), jnp.bfloat16),
+            (8, 128),
+            (8, 128),
+            (128, 144),
+            (144, 128),
+            (200, 16),
+            (16, 192),
+        ],
+        (
+            flow_state,
+            state_tangent,
+            far_field.reshape(1, 5),
+            coordinates,
+            face_neighbour,
+            element_nodes,
+            sends_row,
+            flags_row,
+            damping_row,
+            jnp.asarray(constant_tables()),
+        ),
+        pl.CostEstimate(flops=200_000_000, bytes_accessed=1_000_000, transcendentals=100_000),
+    )
+    residual, table, send_a, send_b, spans, outer, slopes = call(
         main_kernel,
         [
-            (5, 64, 64),
             (5, 64, 64),
             (8, 256),
             (8, 128),
@@ -681,53 +866,63 @@
             (200, 384),
             (5, 48, 128),
             (3, 48, 128),
-            (8, 128),
         ],
-        3,
         (
-            odd,
-            far_field,
-            damping,
-            flow_state,
-            state_tangent,
-            coordinates,
-            face_neighbour,
-            element_nodes,
-            sends_row,
-            flags_row,
+            inner,
+            state,
+            local,
+            places,
+            border,
+            node_index,
+            send_index,
+            named,
+            weight,
+            smoothing,
             got_a,
             got_b,
-            jnp.asarray(assemble),
-            jnp.asarray(assemble.T.copy()),
-            jnp.asarray(corner),
-            jnp.asarray(corner[:192].T.copy()),
+            assemble,
+            transposed,
+            corner,
+            corner_transposed,
         ),
     )
     back_a, back_b = exchange(send_a, send_b, count)
+    change, token = call(
+        change_kernel,
+        [(5, 64, 64), (8, 128)],
+        (inner, state, local, border, got_a, got_b, assemble, spans, outer),
+        pl.CostEstimate(flops=200_000_000, bytes_accessed=1_000_000, transcendentals=100_000),
+    )
+    group = min(16, count)
+    near = [[base + g for g in range(group)] for base in range(0, count, group)]
+    far = [[base + group * g for g in range(count // group)] for base in range(group)]
     descent, sums = call(
         second_kernel,
-        [(3, 128), (1, 128)],
-        2,
+        [(3, 128), (group, 1, 128)],
         (
-            odd,
-            damping,
-            flow_state,
-            element_nodes,
-            sends_row,
-            flags_row,
+            inner,
+            state,
+            node_index,
+            chosen,
+            weight,
+            smoothing,
             table,
             back_a,
             back_b,
             spans,
             outer,
             slopes,
-            jnp.asarray(assemble),
-            jnp.asarray(corner),
+            assemble,
+            corner,
+            token,
         ),
     )
-    total = summed(sums[0], count)
-    step = total[0] / (total[1] + damping[0] * total[0])
-    return (residual, change, step * descent[:, 0:102])
+    sums = lax.all_to_all(sums, "parts", 0, 0, axis_index_groups=near)
+    if count > group:
+        sums = jnp.broadcast_to(jnp.sum(sums, axis=0)[None], (count // group, 1, 128))
+        sums = lax.all_to_all(sums, "parts", 0, 0, axis_index_groups=far)
+    (update,) = call(finish_kernel, [(3, 102)], (sums, descent))
+    return (residual, change, update)
 
 
 def solution(mesh):
@@ -745,4 +940,4 @@
         P("parts"),
     )
     out_specs = (P(None, None, "parts"), P(None, None, "parts"), P(None, "parts"))
-    return jax.shard_map(body, mesh=mesh, in_specs=in_specs, out_specs=out_specs, check_vma=False)
+    return jax.shard_map(step, mesh=mesh, in_specs=in_specs, out_specs=out_specs, check_vma=False)

time: 76.5 us -> 67.2 us (0.88)
  waiting for transfers between devices: 6.64 us -> 2.52 us
  between operations: 2.68 us -> 0.81 us
  local copies, waits for them, and re-layouts: 3.17 us -> 1.69 us
  Pallas kernels: 10.2 us -> 8.91 us
    ppermute x2, waiting for transfers between devices: 6.64 us -> 2.52 us  [exchange(): lax.ppermute(value_b, 'parts', [(i, (i - 1) % count if i % 2 == 0 else (i...]
    pallas_call x3 -> x6, Pallas kernels: 10.2 us -> 8.91 us  [call(): pl.pallas_call(kernel, out_shape=[s if isinstance(s, jax.ShapeDtypeStruct...]
    unnamed x14 -> x20, local copies, waits for them, and re-layouts: 2.51 us -> 1.68 us
  transfers between devices with their start and end apart: 4 -> 4, of which waited for: 2 -> 2; matrix products, arithmetic and copies ran while one was open for 0% -> 0% of each run, Pallas kernels for 0% -> 3%
where the time goes in v1:
time: 67.2 us; the launch traced here: 66.8 us
  blocking collectives  30.5 us (45%)
  starting transfers between devices  22.3 us (33%)
  Pallas kernels  8.91 us (13%)
  waiting for transfers between devices  2.52 us (4%)
  local copies, waits for them, and re-layouts  1.69 us (3%)
  between operations  0.81 us (1%)
    ppermute x2, starting transfers between devices, exchange(): a = lax.ppermute(value_a, 'parts', [(i, i ^ 1) for i in range(count)])  18.5 us
    all_to_all x1, blocking collectives, step(): sums = lax.all_to_all(sums, 'parts', 0, 0, axis_index_groups=far)  15.6 us
    all_to_all x1, blocking collectives, step(): sums = lax.all_to_all(sums, 'parts', 0, 0, axis_index_groups=near)  14.9 us
    pallas_call x6, Pallas kernels, call(): pl.pallas_call(kernel, out_shape=[s if isinstance(s, jax.ShapeDtypeStruct...  8.91 us
    ppermute x2, starting transfers between devices, exchange(): lax.ppermute(value_b, 'parts', [(i, (i - 1) % count if i % 2 == 0 else (i...  3.84 us
    ppermute x2, waiting for transfers between devices, exchange(): lax.ppermute(value_b, 'parts', [(i, (i - 1) % count if i % 2 == 0 else (i...  2.52 us
    unnamed x20, local copies, waits for them, and re-layouts  1.68 us
  transfers between devices with their start and end apart: 4, of which 2 were waited for; matrix products, arithmetic and copies ran while one was open for 0% of the time, Pallas kernels for 3%

profile of v1, /device:TPU:1, one launch (start us, length us, event | category | flops | bytes accessed | tf_op | source)
XLA Modules:
  0.0 66.8 jit_solution(17453055838722259057)
XLA Ops:
  0.7 1.8 %shard_map.140 = (f32[56,128]{1,0:T(8,128)}, f32[56,128]{1,0:T(8,128)}) custom-call(f32[5,64,64]{2,1,0:T(8,128)} %flow_hbm.1, f32[5,64,64]{2,1,0:T(8,128)} %tangent_hbm.1, f32[3,102]{1,0:T(4,128)} %places_hbm.1, s32[1,32]{1,0:T(1,128)} %bitcast.11, s32[1,32]{1,0:T(1,128)} %bitcast.12, s32[1,51]{1,0:T(1,128)} %bitcast.6), custom_call_target="tpu_custom_call" | custom-call | tf_op jit(solution)/shard_map/pallas_call | solution.py:744
  2.4 0.0 copy-start.9
  2.5 0.0 copy-start.4
  2.5 8.7 %collective-permute-start = (f32[56,128]{1,0:T(8,128)}, f32[56,128]{1,0:T(8,128)S(1)}, u32[]{:S(2)}, u32[]{:S(2)}) collective-permute-start(f32[56,128]{1,0:T(8,128)} %get-tuple-element.41), channel_id=1, source_target_pairs={{0,1},{1,0},{2,3},{3,2},{4,5},{5,4},{6,7},{7,6},{8,9},{9,8},{10,11... | collective-permute-start | bytes 86024 | tf_op jit(solution)/shard_map/ppermute | solution.py:764
  11.2 1.9 %collective-permute-start.1 = (f32[56,128]{1,0:T(8,128)}, f32[56,128]{1,0:T(8,128)S(1)}, u32[]{:S(2)}, u32[]{:S(2)}) collective-permute-start(f32[56,128]{1,0:T(8,128)} %get-tuple-element.42), channel_id=1, source_target_pairs={{0,511},{1,2},{2,1},{3,4},{4,3},{5,6},{6,5},{7,8},{8,7},{9,10},{10... | collective-permute-start | bytes 86024 | tf_op jit(solution)/shard_map/ppermute | solution.py:759
  13.1 0.0 copy-start.3
  13.2 0.0 copy-start.6
  13.2 0.0 copy-start.7
  13.2 0.0 copy-start.8
  13.2 0.6 copy-done.3
  13.8 0.0 copy-done.8
  13.9 1.0 %copy-done.2 = f32[488,256]{1,0:T(8,128)S(1)} copy-done((f32[488,256]{1,0:T(8,128)S(1)}, f32[488,256]{1,0:T(8,128)}, u32[]{:S(2)}) %copy-start.2) | copy-done | bytes 499736
  14.9 0.6 shard_map.139
  15.5 0.0 collective-permute-done.a_ref
  15.5 1.1 %collective-permute-done.1.b_ref = f32[56,128]{1,0:T(8,128)S(1)} collective-permute-done((f32[56,128]{1,0:T(8,128)}, f32[56,128]{1,0:T(8,128)S(1)}, u32[]{:S(2)}, u32[]{:S(2)}) %collective-permute-start.1) | collective-permute-done | bytes 28704 | tf_op jit(solution)/shard_map/ppermute | solution.py:759
  16.6 2.6 %shard_map.141 = (f32[5,64,64]{2,1,0:T(8,128)}, f32[8,256]{1,0:T(8,128)S(1)}, f32[8,128]{1,0:T(8,128)S(1)}, f32[8,128]{1,0:T(8,128)S(1)}, f32[200,384]{1,0:T(8,1...) custom-call(f32[10,48,128]{2,1,0:T(8,128)S(1)} %get-tuple-element.31.inner_ref, ...), custom_call_target="tpu_custom_call" | custom-call | tf_op jit(solution)/shard_map/pallas_call | solution.py:744
  19.2 9.7 %collective-permute-start.2 = (f32[8,128]{1,0:T(8,128)S(1)}, f32[8,128]{1,0:T(8,128)S(1)}, u32[]{:S(2)}, u32[]{:S(2)}) collective-permute-start(f32[8,128]{1,0:T(8,128)S(1)} %get-tuple-element.53), channel_id=1, source_target_pairs={{0,1},{1,0},{2,3},{3,2},{4,5},{5,4},{6,7},{7,6},{8,9},{9,8},{10,11... | collective-permute-start | bytes 12296 | tf_op jit(solution)/shard_map/ppermute | solution.py:764
  28.9 1.9 %collective-permute-start.3 = (f32[8,128]{1,0:T(8,128)S(1)}, f32[8,128]{1,0:T(8,128)S(1)}, u32[]{:S(2)}, u32[]{:S(2)}) collective-permute-start(f32[8,128]{1,0:T(8,128)S(1)} %get-tuple-element.54), channel_id=1, source_target_pairs={{0,511},{1,2},{2,1},{3,4},{4,3},{5,6},{6,5},{7,8},{8,7},{9,10},{10... | collective-permute-start | bytes 12296 | tf_op jit(solution)/shard_map/ppermute | solution.py:759
  30.8 1.6 %shard_map.142 = (f32[5,64,64]{2,1,0:T(8,128)}, f32[8,128]{1,0:T(8,128)S(1)}) custom-call(f32[10,48,128]{2,1,0:T(8,128)S(1)} %get-tuple-element.31.inner_ref, f32[10,32,128]{2,1,0:T(8,128)S(1)} %get-tuple-element.32.state_ref, f32[10,48,128]{2,1,0:T(8,128)S(1)} %get-tuple-element.33.local_ref, s32[8,128]{1,0:T(8,128)S(1)} %get-tuple-element.35.border_ref, ...), custom_call_target="tpu_custom_call" | custom-call | flops 200000000 | bytes 1000000 | tf_op jit(solution)/shard_map/pallas_call | solution.py:744
  32.4 1.4 %collective-permute-done.3.b_ref = f32[8,128]{1,0:T(8,128)S(1)} collective-permute-done((f32[8,128]{1,0:T(8,128)S(1)}, f32[8,128]{1,0:T(8,128)S(1)}, u32[]{:S(2)}, u32[]{:S(2)}) %collective-permute-start.3) | collective-permute-done | bytes 4128 | tf_op jit(solution)/shard_map/ppermute | solution.py:759
  33.8 1.7 %shard_map.143 = (f32[3,128]{1,0:T(4,128)S(1)}, f32[16,1,128]{2,1,0:T(1,128)S(1)}) custom-call(f32[10,48,128]{2,1,0:T(8,128)S(1)} %get-tuple-element.31.inner_ref, f32[10,32,128]{2,1,0:T(8,128)S(1)} %get-tuple-element.32.state_ref, s32[8,128]{1,0:T(8,128)S(1)} %get-tuple-element.36.node_index_ref, bf16[128,128]{1,0:T(8,128)(2,1)S(1)} %get-tuple-element.51.chosen_ref, ...), custom_call_target="tpu_custom_call" | custom-call | tf_op jit(solution)/shard_map/pallas_call | solution.py:744
  35.5 14.9 %all_to_all.10 = f32[16,1,128]{2,1,0:T(1,128)S(1)} all-to-all(f32[16,1,128]{2,1,0:T(1,128)S(1)} %get-tuple-element.57), channel_id=1, replica_groups={{0,1,2,3,4,5,6,7,8,9,10,11,12,13,14,15},{16,17,18,19,20,21,22,23,24,25,..., dimensions={0} | all-to-all | bytes 16384 | tf_op jit(solution)/shard_map/all_to_all | solution.py:920
  50.5 15.6 %all_to_all.11.sums_ref = f32[32,1,128]{2,1,0:T(1,128)S(1)} all-to-all(f32[32,1,128]{2,1,0:T(1,128)S(1)} %broadcast_in_dim.2), channel_id=1, replica_groups={{0,16,32,48,64,80,96,112,128,144,160,176,192,208,224,240,256,272,288,30..., dimensions={0} | all-to-all | bytes 32768 | tf_op jit(solution)/shard_map/all_to_all | solution.py:923
  66.1 0.7 %shard_map.144 = f32[3,102]{1,0:T(4,128)} custom-call(f32[32,1,128]{2,1,0:T(1,128)S(1)} %all_to_all.11.sums_ref, f32[3,128]{1,0:T(4,128)S(1)} %get-tuple-element.58.descent_ref), custom_call_target="tpu_custom_call" | custom-call | tf_op jit(solution)/shard_map/pallas_call | solution.py:744
  (14 shorter events, 0.1 us)
Async XLA Ops:
  0.6 12.6 %copy-start = (f32[5,64,64]{2,1,0:T(8,128)S(1)}, f32[5,64,64]{2,1,0:T(8,128)}, u32[]{:S(2)}) copy-start(f32[5,64,64]{2,1,0:T(8,128)} %flow_hbm.1) | copy-start | bytes 245764
  0.6 12.6 %copy-start.1 = (f32[5,64,64]{2,1,0:T(8,128)S(1)}, f32[5,64,64]{2,1,0:T(8,128)}, u32[]{:S(2)}) copy-start(f32[5,64,64]{2,1,0:T(8,128)} %tangent_hbm.1) | copy-start | bytes 245764
  0.7 12.6 %copy-start.5 = (s32[8,64]{1,0:T(8,128)S(1)}, s32[8,64]{1,0:T(8,128)}, u32[]{:S(2)}) copy-start(s32[8,64]{1,0:T(8,128)} %nodes_ref.1) | copy-start | bytes 6148
  2.4 10.8 %copy-start.9 = (f32[2]{0:T(128)S(1)}, f32[2]{0:T(128)}, u32[]{:S(2)}) copy-start(f32[2]{0:T(128)} %param.16) | copy-start | bytes 28
  2.5 10.8 %copy-start.4 = (s32[6,64]{1,0:T(8,128)S(1)}, s32[6,64]{1,0:T(8,128)}, u32[]{:S(2)}) copy-start(s32[6,64]{1,0:T(8,128)} %neighbour_ref.1) | copy-start | bytes 4612
  2.5 13.0 %collective-permute-start = (f32[56,128]{1,0:T(8,128)}, f32[56,128]{1,0:T(8,128)S(1)}, u32[]{:S(2)}, u32[]{:S(2)}) collective-permute-start(f32[56,128]{1,0:T(8,128)} %get-tuple-element.41), channel_id=1, source_target_pairs={{0,1},{1,0},{2,3},{3,2},{4,5},{5,4},{6,7},{7,6},{8,9},{9,8},{10,11... | collective-permute-start | bytes 86024 | tf_op jit(solution)/shard_map/ppermute | solution.py:764
  11.2 5.4 %collective-permute-start.1 = (f32[56,128]{1,0:T(8,128)}, f32[56,128]{1,0:T(8,128)S(1)}, u32[]{:S(2)}, u32[]{:S(2)}) collective-permute-start(f32[56,128]{1,0:T(8,128)} %get-tuple-element.42), channel_id=1, source_target_pairs={{0,511},{1,2},{2,1},{3,4},{4,3},{5,6},{6,5},{7,8},{8,7},{9,10},{10... | collective-permute-start | bytes 86024 | tf_op jit(solution)/shard_map/ppermute | solution.py:759
  13.1 0.7 %copy-start.3 = (f32[3,102]{1,0:T(4,128)S(1)}, f32[3,102]{1,0:T(4,128)}, u32[]{:S(2)}) copy-start(f32[3,102]{1,0:T(4,128)} %places_hbm.1) | copy-start | bytes 3676
  13.2 0.7 %copy-start.6 = (s32[51]{0:T(128)S(1)}, s32[51]{0:T(128)}, u32[]{:S(2)}) copy-start(s32[51]{0:T(128)} %param.21) | copy-start | bytes 616
  13.2 0.7 copy-start.7
  13.2 0.7 %copy-start.8 = (s32[64]{0:T(128)S(1)}, s32[64]{0:T(128)}, u32[]{:S(2)}) copy-start(s32[64]{0:T(128)} %param.22) | copy-start | bytes 772
  13.9 1.0 %copy-start.2 = (f32[488,256]{1,0:T(8,128)S(1)}, f32[488,256]{1,0:T(8,128)}, u32[]{:S(2)}) copy-start(f32[488,256]{1,0:T(8,128)} %constant.4.clone.tables_ref) | copy-start | bytes 1499140
  19.2 13.2 %collective-permute-start.2 = (f32[8,128]{1,0:T(8,128)S(1)}, f32[8,128]{1,0:T(8,128)S(1)}, u32[]{:S(2)}, u32[]{:S(2)}) collective-permute-start(f32[8,128]{1,0:T(8,128)S(1)} %get-tuple-element.53), channel_id=1, source_target_pairs={{0,1},{1,0},{2,3},{3,2},{4,5},{5,4},{6,7},{7,6},{8,9},{9,8},{10,11... | collective-permute-start | bytes 12296 | tf_op jit(solution)/shard_map/ppermute | solution.py:764
  28.9 4.9 %collective-permute-start.3 = (f32[8,128]{1,0:T(8,128)S(1)}, f32[8,128]{1,0:T(8,128)S(1)}, u32[]{:S(2)}, u32[]{:S(2)}) collective-permute-start(f32[8,128]{1,0:T(8,128)S(1)} %get-tuple-element.54), channel_id=1, source_target_pairs={{0,511},{1,2},{2,1},{3,4},{4,3},{5,6},{6,5},{7,8},{8,7},{9,10},{10... | collective-permute-start | bytes 12296 | tf_op jit(solution)/shard_map/ppermute | solution.py:759

commit v2 on v1

--- a/solution.py
+++ b/solution.py
@@ -246,52 +246,54 @@
     return result
 
 
-def on_odd():
-    return (lax.axis_index("parts") & 1) == 1
-
-
-def pack_kernel(
-    flow_hbm,
-    tangent_hbm,
-    places_hbm,
-    upper_hbm,
-    lower_hbm,
-    nodes_hbm,
-    a_ref,
-    b_ref,
-    flow_ref,
-    tangent_ref,
-    places_ref,
-    upper_ref,
-    lower_ref,
-    nodes_ref,
-    semaphores,
-):
-    copies = [
-        (flow_hbm.at[:, 0:16, :], flow_ref.at[:, 0:16, :]),
-        (flow_hbm.at[:, 48:64, :], flow_ref.at[:, 16:32, :]),
-        (tangent_hbm.at[:, 0:16, :], tangent_ref.at[:, 0:16, :]),
-        (tangent_hbm.at[:, 48:64, :], tangent_ref.at[:, 16:32, :]),
-        (places_hbm, places_ref),
-        (upper_hbm, upper_ref),
-        (lower_hbm, lower_ref),
-        (nodes_hbm, nodes_ref),
-    ]
+def position_bit(bit):
+    return ((lax.axis_index("parts") >> bit) & 1) == 1
+
+
+def pack_kernel(*refs):
+    sources = refs[0:10]
+    tables_hbm, damping_hbm = refs[10:12]
+    (
+        a_ref,
+        b_ref,
+        c_ref,
+        d_ref,
+        up_ref,
+        down_ref,
+        flagged_ref,
+        sends_out,
+        tables_out,
+        damping_out,
+    ) = refs[12:22]
+    held = refs[22:32]
+    semaphores = refs[32]
+    moves = list(zip(sources, held)) + [(tables_hbm, tables_out), (damping_hbm, damping_out)]
     copies = [
         pltpu.make_async_copy(source, target, semaphores.at[i])
-        for i, (source, target) in enumerate(copies)
+        for i, (source, target) in enumerate(moves)
     ]
     for copy in copies:
         copy.start()
-    for copy in copies:
+    for copy in copies[0:10]:
         copy.wait()
-    odd = on_odd()
+    (
+        flow_ref,
+        tangent_ref,
+        places_ref,
+        upper_ref,
+        lower_ref,
+        sends_ref,
+        neighbour_ref,
+        nodes_ref,
+        flags_ref,
+        far_ref,
+    ) = held
     lane = lanes()
     group = lane // 32
+    group16 = jnp.concatenate([group, group], axis=0)
 
     def faces(list_ref, row):
-        index = pad_lanes(list_ref[...])
-        index = spread(index)
+        index = spread(pad_lanes(list_ref[...]))
         tiled = index
         for g in range(1, 4):
             tiled = jnp.where(group == g, pltpu.roll(index, 32 * g, 1), tiled)
@@ -303,23 +305,104 @@
                 if v >= 10:
                     continue
                 source = flow_ref if v < 5 else tangent_ref
-                block = pad_lanes(source[v % 5, row : row + 16, :])
-                block = pick(block, tiled)
-                own = jnp.concatenate([group, group], axis=0) == g
-                merged = jnp.where(own, block, 0.0 if merged is None else merged)
+                block = pick(pad_lanes(source[v % 5, row : row + 16, :]), tiled)
+                merged = jnp.where(group16 == g, block, 0.0 if merged is None else merged)
             chunks.append(merged)
         return jnp.concatenate(chunks, axis=0)
 
-    up = faces(upper_ref, 16)
+    up = faces(upper_ref, 48)
     down = faces(lower_ref, 0)
-    node_index = spread(pad_lanes(nodes_ref[...]))
-    places = jnp.concatenate([places_ref[...], jnp.zeros((5, 102), F32)], axis=0)
-    nodes = pick(pad_lanes(places), node_index)
+    sends_row = pad_lanes(sends_ref[...])
+    places = pad_lanes(jnp.concatenate([places_ref[...], jnp.zeros((5, 102), F32)], axis=0))
+    nodes = pick(places, spread(sends_row))
+    row8 = lax.broadcasted_iota(jnp.int32, (8, 128), 0)
+    nodes = jnp.where(row8 == 3, spread(sends_row.astype(F32)), nodes)
     none = jnp.zeros((8, 128), F32)
     up = jnp.concatenate([up, none], axis=0)
     down = jnp.concatenate([down, nodes], axis=0)
-    a_ref[...] = jnp.where(odd, down, up)
-    b_ref[...] = jnp.where(odd, up, down)
+
+    flags = pad_lanes(flags_ref[...].astype(F32))
+    first_row = lax.broadcasted_iota(jnp.int32, (64, 128), 0)
+    rank = jnp.sum(
+        jnp.where(lanes(64) <= first_row, jnp.broadcast_to(flags, (64, 128)), 0.0),
+        axis=1,
+        keepdims=True,
+    )
+    wanted = (lane % 16).astype(F32)
+    before = jnp.sum((rank <= wanted[0:1]).astype(F32), axis=0, keepdims=True)
+    weight = (before < 63.5).astype(F32)
+    chosen = spread(jnp.minimum(before, 63.0).astype(jnp.int32))
+    block = lane // 16
+
+    def merged_blocks(parts):
+        result = parts[0]
+        for b, part in enumerate(parts[1:]):
+            result = jnp.where(block == b + 1, part, result)
+        return result
+
+    neighbours = neighbour_ref[...]
+    listed = [
+        spread(pair(neighbours[2 * j : 2 * j + 1], neighbours[2 * j + 1 : 2 * j + 2]))
+        for j in range(3)
+    ]
+    beside = []
+    for j in range(3):
+        sides = []
+        for side in range(2):
+            code = pick(listed[j], chosen + 64 * side)
+            local = jnp.where(code < 64, code, 0) + (64 if side == 0 else 0)
+            sides.append((code == 96, local))
+        beside.append(sides)
+    packed = []
+    for v in range(5):
+        value = pad_lanes(flow_ref[v])
+        packed.append(
+            merged_blocks([pick(value[8 * b : 8 * b + 8], chosen) for b in range(8)])
+        )
+    for v in range(5):
+        inner = face_pairs(flow_ref, v)
+        far_value = far_ref[0:1, v : v + 1]
+        for first in (0, 4):
+            parts = []
+            for b in range(8):
+                chunk, side = first + b % 4, b // 4
+                if chunk >= 6:
+                    parts.append(none)
+                    continue
+                far, local = beside[chunk // 2][side]
+                taken = pick(inner[8 * chunk : 8 * chunk + 8], local)
+                parts.append(jnp.where(far, far_value, taken))
+            packed.append(merged_blocks(parts))
+    node_index = pick(pair(nodes_ref[...], nodes_ref[...]), chosen)
+    local_node = jnp.where(node_index < 102, node_index, 0)
+    codes = jnp.where(
+        row8 == 0,
+        pick(listed[0], chosen).astype(F32),
+        jnp.where(row8 == 1, pick(listed[0], chosen + 64).astype(F32), spread(weight)),
+    )
+    packed.append(
+        merged_blocks(
+            [pick(spread(places[i : i + 1]), local_node) for i in range(3)]
+            + [node_index.astype(F32), codes]
+        )
+    )
+    flagged = jnp.concatenate(packed, axis=0)
+    flagged_ref[...] = flagged
+    sends_out[...] = sends_ref[...]
+    up_ref[...] = up
+    down_ref[...] = down
+    odd = position_bit(0)
+    second = position_bit(1)
+    a_ref[0:56] = jnp.where(odd, down, up)
+    b_ref[0:56] = jnp.where(odd, up, down)
+    a_ref[56:184] = flagged
+    b_ref[56:184] = flagged
+    short_up = jnp.concatenate([up[0:32], up[48:56]], axis=0)
+    short_down = jnp.concatenate([down[0:32], down[48:56]], axis=0)
+    c_ref[...] = jnp.where(second, short_down, short_up)
+    d_ref[...] = jnp.where(second, short_up, short_down)
+    for copy in copies[10:12]:
+        copy.wait()
 
 
 def face_pairs(ref, v):
@@ -387,9 +470,6 @@
     places_ref,
     neighbour_ref,
     nodes_ref,
-    sends_ref,
-    flags_ref,
-    damping_ref,
     tables_ref,
     inner_ref,
     state_ref,
@@ -397,15 +477,8 @@
     places_out,
     border_ref,
     node_index_ref,
-    send_index_ref,
-    named_ref,
-    chosen_ref,
-    weight_ref,
-    smoothing_ref,
     assemble_ref,
-    transposed_ref,
     corner_ref,
-    corner_transposed_ref,
 ):
     lane = lanes()
     low = lane < 64
@@ -432,32 +505,8 @@
     places_out[...] = jnp.concatenate([pad_lanes(places_ref[...]), jnp.zeros((5, 128), F32)], axis=0)
     node_index = pair(nodes_ref[...], nodes_ref[...])
     node_index_ref[...] = node_index
-    send_row = pad_lanes(sends_ref[...])
-    send_index_ref[...] = spread(send_row)
-    table_row = lax.broadcasted_iota(jnp.int32, (256, 128), 0)
-    node_of_row = jnp.where(
-        table_row < 102, table_row, jnp.where(table_row < 128, -1, table_row - 26)
-    )
-    for p in range(4):
-        named = jnp.where(
-            low[0:1], node_index[2 * p : 2 * p + 1], node_index[2 * p + 1 : 2 * p + 2]
-        )
-        named_ref[:, 128 * p : 128 * p + 128] = (
-            (node_of_row == named).astype(F32).astype(jnp.bfloat16)
-        )
-    sent = jnp.where(lane[0:1] < 51, send_row, -1)
-    chosen_ref[...] = (
-        (lax.broadcasted_iota(jnp.int32, (128, 128), 0) == sent).astype(F32).astype(jnp.bfloat16)
-    )
-    weight = flags_ref[...].astype(F32)
-    weight_ref[...] = spread(pair(weight, weight))
-    smoothing_ref[...] = jnp.where(
-        lane == 0, damping_ref[0:1, 0:1], jnp.broadcast_to(damping_ref[0:1, 1:2], (8, 128))
-    )
     assemble_ref[...] = tables_ref[0:128, 0:144]
-    transposed_ref[...] = tables_ref[128:272, 0:128]
     corner_ref[...] = tables_ref[272:472, 0:16]
-    corner_transposed_ref[...] = tables_ref[472:488, 0:192]
 
 
 class Border:
@@ -500,95 +549,143 @@
     return [folded(product, v) for v in range(5)]
 
 
-def change_kernel(
-    inner_ref,
-    state_ref,
-    local_ref,
-    border_ref,
-    a_ref,
-    b_ref,
-    assemble_ref,
-    spans_ref,
-    outer_ref,
-    change_ref,
-    token_ref,
-):
-    odd = on_odd()
-    from_a = a_ref[...]
-    from_b = b_ref[...]
-    border = Border(border_ref[...], jnp.where(odd, from_a, from_b), jnp.where(odd, from_b, from_a))
-    volume_spans, face_spans = tangents_of(spans_ref[...])
-    normals, face_normal, area_square, area = geometry(volume_spans, face_spans)
-    inner = [inner_ref[v] for v in range(5)]
-    inner_change = [inner_ref[5 + v] for v in range(5)]
-    outer = [outer_ref[v] for v in range(5)]
-    outer_change = [border.values(local_ref[5 + v], 5 + v) for v in range(5)]
-    _, jump_change = jax.jvp(
-        lambda u, w: jump_of(u, w, face_normal, area_square, area),
-        (inner, outer),
-        (inner_change, outer_change),
-    )
-    state = [state_ref[v] for v in range(5)]
-    state_change = [state_ref[5 + v] for v in range(5)]
-    _, flux_changes = jax.jvp(lambda u: volume_flux(u, normals), (state,), (state_change,))
-    change = assembled(assemble_ref[...], flux_changes, jump_change)
-    for v in range(5):
-        change_ref[v] = change[v][:, 0:64]
-    token_ref[...] = jnp.zeros((8, 128), F32)
-
-
-def main_kernel(
+def plane_kernel(
     inner_ref,
     state_ref,
     local_ref,
     places_ref,
     border_ref,
     node_index_ref,
-    send_index_ref,
-    named_ref,
-    weight_ref,
-    smoothing_ref,
     a_ref,
     b_ref,
     assemble_ref,
-    transposed_ref,
     corner_ref,
-    corner_transposed_ref,
     residual_ref,
-    table_ref,
-    send_a_ref,
-    send_b_ref,
-    spans_ref,
-    outer_ref,
-    slopes_ref,
+    change_ref,
 ):
-    odd = on_odd()
-    lane = lanes()
-    from_a = a_ref[...]
-    from_b = b_ref[...]
+    odd = position_bit(0)
+    from_a = a_ref[0:56]
+    from_b = b_ref[0:56]
     lower = jnp.where(odd, from_a, from_b)
     upper = jnp.where(odd, from_b, from_a)
-
+    border = Border(border_ref[...], lower, upper)
     corners = corner_values(node_index_ref[...], places_ref[...], upper[48:56])
-    relative = [c - c[0:1] for c in corners]
-    spans = dot(corner_ref[...], corner_operand(relative))
-    spans_ref[...] = spans
+    spans = dot(corner_ref[...], corner_operand([c - c[0:1] for c in corners]))
+    volume_spans, face_spans = tangents_of(spans)
+    normals, face_normal, area_square, area = geometry(volume_spans, face_spans)
+    inner = [inner_ref[v] for v in range(10)]
+    outer = [border.values(local_ref[v], v) for v in range(10)]
+    jump, jump_change = jax.jvp(
+        lambda u, w: jump_of(u, w, face_normal, area_square, area),
+        (inner[:5], outer[:5]),
+        (inner[5:], outer[5:]),
+    )
+    state = [state_ref[v] for v in range(10)]
+    fluxes, flux_changes = jax.jvp(
+        lambda u: volume_flux(u, normals), (state[:5],), (state[5:],)
+    )
+    residual = assembled(assemble_ref[...], fluxes, jump)
+    change = assembled(assemble_ref[...], flux_changes, jump_change)
+    for v in range(5):
+        residual_ref[v] = residual[v][:, 0:64]
+        change_ref[v] = change[v][:, 0:64]
+
+
+def core_kernel(
+    a_ref,
+    b_ref,
+    c_ref,
+    d_ref,
+    up_ref,
+    down_ref,
+    flagged_ref,
+    sends_ref,
+    tables_ref,
+    damping_ref,
+    descent_ref,
+    sums_ref,
+    whole_ref,
+):
+    odd = position_bit(0)
+    second = position_bit(1)
+    lower = jnp.where(odd, a_ref[...], b_ref[...])
+    upper = jnp.where(odd, b_ref[...], a_ref[...])
+    lower_two = jnp.where(second, c_ref[...], d_ref[...])
+    upper_two = jnp.where(second, d_ref[...], c_ref[...])
+    up = up_ref[...]
+    down = down_ref[...]
+    flagged = flagged_ref[...]
+    lane = lanes()
+    low = lane < 64
+    seat = lane % 16
+    block = (lane % 64) // 16
+
+    def three(own, below, above):
+        return jnp.where(block == 1, below, jnp.where(block == 2, above, own))
+
+    def taken(row, index):
+        rows = slice(row, row + 8)
+        moved = slice(56 + row, 64 + row)
+        return three(
+            pick(flagged[rows], index), pick(lower[moved], index), pick(upper[moved], index)
+        )
+
+    for v in range(5):
+        for r in range(8):
+            whole_ref[v, 8 * r : 8 * r + 8, :] = taken(8 * v, seat + 16 * r)
+    state = []
+    inner = []
+    for v in range(5):
+        value = whole_ref[v]
+        state.append(jnp.where(lanes(32) < 64, value[0:32], value[32:64]))
+        sides = []
+        for s in range(2):
+            middle = jnp.concatenate(
+                [value[16 * i + 12 * s : 16 * i + 12 * s + 4] for i in range(4)], axis=0
+            )
+            last = whole_ref[pl.ds(v, 1), pl.ds(3 * s, 16, stride=4), :][0]
+            sides.append(jnp.concatenate([value[48 * s : 48 * s + 16], middle, last], axis=0))
+        inner.append(jnp.where(lanes(48) < 64, sides[0], sides[1]))
+    codes = taken(120, seat + 64)
+    border = spread(jnp.where(low[0:1], codes[0:1], codes[1:2])).astype(jnp.int32)
+    weight = jnp.where(block[0:1] == 3, 0.0, codes[2:3])
+    slot = jnp.clip(border - 64, 0, 31)
+    halo = (border >= 64) & (border < 96)
+    outer = []
+    for v in range(5):
+        chunks = []
+        for chunk in range(6):
+            index = seat + 16 * (chunk % 4) + jnp.where(low, 0, 64)
+            value = taken(40 + 16 * v + 8 * (chunk // 4), index)
+            if chunk < 2:
+                rows = slice(16 * (v // 4) + 8 * chunk, 16 * (v // 4) + 8 * chunk + 8)
+                at = slot + 32 * (v % 4)
+                side0 = three(pick(lower[rows], at), pick(lower_two[rows], at), pick(up[rows], at))
+                side1 = three(
+                    pick(upper[rows], at), pick(down[rows], at), pick(upper_two[rows], at)
+                )
+                value = jnp.where(halo, jnp.where(low, side0, side1), value)
+            chunks.append(value)
+        outer.append(jnp.concatenate(chunks, axis=0))
+    node_index = taken(120, seat + 48).astype(jnp.int32)
+    foreign = node_index >= 102
+    foreign_slot = jnp.where(foreign, node_index - 102, 0)
+    corners = []
+    for i in range(3):
+        local = taken(120, seat + 16 * i)
+        remote = three(
+            pick(spread(upper[48 + i : 49 + i]), foreign_slot),
+            pick(spread(down[48 + i : 49 + i]), foreign_slot),
+            pick(spread(upper_two[32 + i : 33 + i]), foreign_slot),
+        )
+        corners.append(jnp.where(foreign, remote, local))
+
+    spans = dot(tables_ref[272:472, 0:16], corner_operand([c - c[0:1] for c in corners]))
     volume_spans, face_spans = tangents_of(spans)
     normals, face_normal, area_square, area = geometry(volume_spans, face_spans)
     sign = side_sign()
-
-    inner = [inner_ref[v] for v in range(5)]
-    border = Border(border_ref[...], lower, upper)
-    outer = [border.values(local_ref[v], v) for v in range(5)]
-    for v in range(5):
-        outer_ref[v] = outer[v]
     jump = jump_of(inner, outer, face_normal, area_square, area)
-    state = [state_ref[v] for v in range(5)]
-    residual = assembled(assemble_ref[...], volume_flux(state, normals), jump)
-    for v in range(5):
-        residual_ref[v] = residual[v][:, 0:64]
-
-    weight = weight_ref[0:1]
+    residual = assembled(tables_ref[0:128, 0:144], volume_flux(state, normals), jump)
     low64 = lanes(64) < 64
     seeds = []
     for v in range(5):
@@ -599,7 +696,7 @@
                 axis=0,
             )
         )
-    back = dot(transposed_ref[...], jnp.concatenate(seeds, axis=1))
+    back = dot(tables_ref[128:272, 0:128], jnp.concatenate(seeds, axis=1))
     prims = primitives(state)
     normal_bar = []
     for j in range(3):
@@ -609,8 +706,6 @@
     inner_prims = primitives(inner)
     outer_prims = primitives(outer)
     slopes = wave_gradient(inner_prims, outer_prims, face_normal, area_square, area)
-    for i in range(3):
-        slopes_ref[i] = slopes[i]
     lift = sum(c * (w - u) for c, w, u in zip(cotangent, outer, inner))
     from_outer = along_flux_transposed(outer_prims, cotangent)
     from_inner = along_flux_transposed(inner_prims, cotangent)
@@ -633,12 +728,12 @@
         ],
         axis=1,
     )
-    corner_bar = dot(corner_transposed_ref[...], stacked_bar)
-    smoothing = smoothing_ref[0:1, 1:2]
+    corner_bar = dot(tables_ref[472:488, 0:192], stacked_bar)
+    smoothing = damping_ref[0:1, 1:2]
     pieces = []
     for i in range(3):
-        block = columns(corner_bar, slice(0, 16), i)
-        bar = block[0:8] + pltpu.roll(block[8:16], 64, 1)
+        halves = columns(corner_bar, slice(0, 16), i)
+        bar = halves[0:8] + pltpu.roll(halves[8:16], 64, 1)
         bar = bar + smoothing * weight * columns(spans, slice(192, 200), i)
         pieces.append(bar)
     pieces.append(spread(weight))
@@ -646,88 +741,78 @@
     gradient = jnp.where(lanes(32) < 64, gradient, pltpu.roll(gradient, 64, 1))
     row_corner = lax.broadcasted_iota(jnp.int32, (32, 128), 0) % 8
     half = jnp.where(lanes(32) < 64, 0, 1)
-    left = [jnp.where(row_corner == 2 * p + half, gradient, 0.0) for p in range(4)]
-    scattered = placed(jnp.concatenate(left, axis=1), named_ref[...])
+    sent_here = pick(spread(pad_lanes(sends_ref[...])), foreign_slot)
+    nowhere = jnp.full((8, 128), -1, jnp.int32)
+    own_node = three(
+        jnp.where(foreign, -1, node_index), jnp.where(foreign, sent_here, -1), nowhere
+    )
+    own_node = jnp.where(block == 3, -1, own_node)
+    halo_node = jnp.where(block == 0, jnp.where(foreign, node_index - 102, -1), nowhere)
+    upper_node = jnp.where((block == 2) & ~foreign, node_index, -1)
+    square_row = lax.broadcasted_iota(jnp.int32, (128, 128), 0)
+    upper_sends = jnp.where(lane[0:1] < 51, upper[51:52], -5.0)
+    upper_column = jnp.sum(
+        jnp.where(square_row == lanes(128), jnp.broadcast_to(upper_sends, (128, 128)), 0.0),
+        axis=1,
+        keepdims=True,
+    ).astype(jnp.int32)
+    left = []
+    right = []
+    for p in range(4):
+        left.append(jnp.where(row_corner == 2 * p + half, gradient, 0.0))
+
+        def row_of(index):
+            return jnp.where(low[0:1], index[2 * p : 2 * p + 1], index[2 * p + 1 : 2 * p + 2])
+
+        own_hit = square_row == row_of(own_node)
+        halo_hit = (square_row == row_of(halo_node)) | (upper_column == row_of(upper_node))
+        right.append(
+            jnp.concatenate([own_hit.astype(F32), halo_hit.astype(F32)], axis=0).astype(
+                jnp.bfloat16
+            )
+        )
+    scattered = placed(jnp.concatenate(left, axis=1), jnp.concatenate(right, axis=1))
     rows = [jnp.sum(scattered[8 * i : 8 * i + 8], axis=0, keepdims=True) for i in range(4)]
     table = jnp.concatenate(rows + [jnp.zeros((4, 256), F32)], axis=0)
-    table_ref[...] = table
-    up = table[:, 128:256]
-    down = jnp.where(lane < 51, pick(table[:, 0:128], send_index_ref[...]), 0.0)
-    send_a_ref[...] = jnp.where(odd, down, up)
-    send_b_ref[...] = jnp.where(odd, up, down)
-
-
-def second_kernel(
-    inner_ref,
-    state_ref,
-    node_index_ref,
-    chosen_ref,
-    weight_ref,
-    smoothing_ref,
-    table_ref,
-    a_ref,
-    b_ref,
-    spans_ref,
-    outer_ref,
-    slopes_ref,
-    assemble_ref,
-    corner_ref,
-    _,
-    descent_ref,
-    sums_ref,
-):
-    odd = on_odd()
-    lane = lanes()
-    from_a = a_ref[...]
-    from_b = b_ref[...]
-    lower = jnp.where(odd, from_a, from_b)
-    upper = jnp.where(odd, from_b, from_a)
-    table = table_ref[...]
-    sixteen = jnp.concatenate([jnp.where(lane < 51, lower, 0.0), jnp.zeros((8, 128), F32)], axis=0)
-    own = table[:, 0:128] + placed(sixteen, chosen_ref[...])[0:8]
-    halo = table[:, 128:256] + upper
+    own = table[:, 0:128]
+    halo_table = table[:, 128:256]
     own = -jnp.where(own[3:4] > 0.5, own, 0.0)
-    halo = -jnp.where(halo[3:4] > 0.5, halo, 0.0)
+    halo_table = -jnp.where(halo_table[3:4] > 0.5, halo_table, 0.0)
     descent_ref[...] = own[0:3]
     moved = jnp.where(lax.broadcasted_iota(jnp.int32, (8, 128), 0) < 3, own, 0.0)
     norm = jnp.sum(moved * moved, axis=(0, 1), keepdims=True)
 
-    steps = corner_values(node_index_ref[...], own, halo)
-    moves = dot(corner_ref[...], corner_operand(steps))
+    steps = corner_values(node_index, own, halo_table)
+    moves = dot(tables_ref[272:472, 0:16], corner_operand(steps))
     volume_moves, face_moves = tangents_of(moves)
-    volume_spans, face_spans = tangents_of(spans_ref[...])
-    state = primitives([state_ref[v] for v in range(5)])
     fluxes = []
     for j in range(3):
         a, b = (j + 1) % 3, (j + 2) % 3
         normal_move = added(
             cross(volume_moves[a], volume_spans[b]), cross(volume_spans[a], volume_moves[b])
         )
-        fluxes.append(along_flux(state, normal_move))
-    sign = side_sign()
+        fluxes.append(along_flux(prims, normal_move))
     face_move = [
         sign * n
         for n in added(cross(face_moves[0], face_spans[1]), cross(face_spans[0], face_moves[1]))
     ]
-    inner = [inner_ref[v] for v in range(5)]
-    outer = [outer_ref[v] for v in range(5)]
-    inner_flux = along_flux(primitives(inner), face_move)
-    outer_flux = along_flux(primitives(outer), face_move)
-    wave_move = sum(slopes_ref[i] * face_move[i] for i in range(3))
+    inner_flux = along_flux(inner_prims, face_move)
+    outer_flux = along_flux(outer_prims, face_move)
+    wave_move = sum(slopes[i] * face_move[i] for i in range(3))
     jump = [
         0.5 * (outer_flux[v] - inner_flux[v] - wave_move * (outer[v] - inner[v]))
         for v in range(5)
     ]
-    square = sum(
-        change * change for change in assembled(assemble_ref[...], fluxes, jump)
-    )
-    weight = jnp.where(lane[0:1] < 64, weight_ref[0:1], 0.0)
-    curvature = jnp.sum(jnp.sum(square, axis=0, keepdims=True) * weight, axis=1, keepdims=True)
+    square = sum(change * change for change in assembled(tables_ref[0:128, 0:144], fluxes, jump))
+    own_weight = jnp.where(lane[0:1] < 16, weight, 0.0)
+    curvature = jnp.sum(
+        jnp.sum(square, axis=0, keepdims=True) * own_weight, axis=1, keepdims=True
+    )
     bend = sum(steps[i] * columns(moves, slice(192, 200), i) for i in range(3))
-    bending = smoothing_ref[0:1, 1:2] * jnp.sum(
-        jnp.sum(bend, axis=0, keepdims=True) * weight, axis=1, keepdims=True
-    )
-    lower_sum = curvature + bending + smoothing_ref[0:1, 0:1] * norm
+    bending = smoothing * jnp.sum(
+        jnp.sum(bend, axis=0, keepdims=True) * own_weight, axis=1, keepdims=True
+    )
+    lower_sum = curvature + bending + damping_ref[0:1, 0:1] * norm
     sums = jnp.where(lane[0:1] == 0, norm, jnp.where(lane[0:1] == 1, lower_sum, 0.0))
     for i in range(sums_ref.shape[0]):
         sums_ref[i] = sums
@@ -739,7 +824,7 @@
     update_ref[...] = step * descent_ref[:, 0:102]
 
 
-def call(kernel, out_shape, arrays, cost=None, place=pltpu.VMEM, scratch=(), limit=16 << 20):
+def call(kernel, out_shape, arrays, cost=None, places=None, scratch=(), limit=16 << 20):
     vector = pl.BlockSpec(memory_space=pltpu.VMEM)
     return pl.pallas_call(
         kernel,
@@ -747,7 +832,7 @@
             s if isinstance(s, jax.ShapeDtypeStruct) else jax.ShapeDtypeStruct(s, F32)
             for s in out_shape
         ],
-        in_specs=[pl.BlockSpec(memory_space=place)] * len(arrays),
+        in_specs=[pl.BlockSpec(memory_space=p) for p in places or [pltpu.VMEM] * len(arrays)],
         out_specs=[vector] * len(out_shape),
         scratch_shapes=list(scratch),
         compiler_params=pltpu.CompilerParams(vmem_limit_bytes=limit),
@@ -755,14 +840,21 @@
     )(*arrays)
 
 
-def exchange(value_a, value_b, count):
-    b = lax.ppermute(
-        value_b,
-        "parts",
-        [(i, (i - 1) % count if i % 2 == 0 else (i + 1) % count) for i in range(count)],
-    )
-    a = lax.ppermute(value_a, "parts", [(i, i ^ 1) for i in range(count)])
-    return a, b
+def beyond(i, count):
+    return (i - 1) % count if i % 2 == 0 else (i + 1) % count
+
+
+def beyond_two(i, count):
+    return (i - 2) % count if i // 2 % 2 == 0 else (i + 2) % count
+
+
+def swapped(value, partner):
+    count = lax.axis_size("parts")
+    return lax.ppermute(value, "parts", [(i, partner(i)) for i in range(count)])
+
+
+def stays(value):
+    return pltpu.with_memory_space_constraint(value, pltpu.HBM)
 
 
 def step(
@@ -783,30 +875,47 @@
     flags_row = shock_flags.reshape(1, 64)
     damping_row = damping.reshape(1, 2)
     integer = jnp.int32
-    pack_a, pack_b = call(
+    tables = jnp.asarray(constant_tables())
+    pack_a, pack_b, pack_c, pack_d, up, down, flagged, sends, held_tables, held_damping = call(
         pack_kernel,
-        [(56, 128)] * 2,
-        (
-            flow_state,
-            state_tangent,
-            coordinates,
-            upper_sends.reshape(1, 32),
-            lower_sends.reshape(1, 32),
-            sends_row,
+        [(184, 128)] * 2 + [(40, 128)] * 2 + [(56, 128)] * 2
+        + [(128, 128), jax.ShapeDtypeStruct((1, 51), integer), (488, 256), (1, 2)],
+        tuple(
+            stays(x)
+            for x in (
+                flow_state,
+                state_tangent,
+                coordinates,
+                upper_sends.reshape(1, 32),
+                lower_sends.reshape(1, 32),
+                sends_row,
+                face_neighbour,
+                element_nodes,
+                flags_row,
+                far_field.reshape(1, 5),
+                tables,
+                damping_row,
+            )
         ),
-        place=pltpu.HBM,
-        limit=60 * 1024 * 1024,
+        places=[pltpu.HBM] * 12,
         scratch=(
-            pltpu.VMEM((5, 32, 64), F32),
-            pltpu.VMEM((5, 32, 64), F32),
+            pltpu.VMEM((5, 64, 64), F32),
+            pltpu.VMEM((5, 64, 64), F32),
             pltpu.VMEM((3, 102), F32),
             pltpu.VMEM((1, 32), integer),
             pltpu.VMEM((1, 32), integer),
             pltpu.VMEM((1, 51), integer),
-            pltpu.SemaphoreType.DMA((8,)),
+            pltpu.VMEM((6, 64), integer),
+            pltpu.VMEM((8, 64), integer),
+            pltpu.VMEM((1, 64), integer),
+            pltpu.VMEM((1, 5), F32),
+            pltpu.SemaphoreType.DMA((12,)),
         ),
     )
-    got_a, got_b = exchange(pack_a, pack_b, count)
+    got_d = swapped(pack_d, lambda i: beyond_two(i, count))
+    got_b = swapped(pack_b, lambda i: beyond(i, count))
+    got_c = swapped(pack_c, lambda i: i ^ 2)
+    got_a = swapped(pack_a, lambda i: i ^ 1)
     (
         inner,
         state,
@@ -814,15 +923,8 @@
         places,
         border,
         node_index,
-        send_index,
-        named,
-        chosen,
-        weight,
-        smoothing,
         assemble,
-        transposed,
         corner,
-        corner_transposed,
     ) = call(
         ready_kernel,
         [
@@ -832,15 +934,8 @@
             (8, 128),
             jax.ShapeDtypeStruct((8, 128), integer),
             jax.ShapeDtypeStruct((8, 128), integer),
-            jax.ShapeDtypeStruct((8, 128), integer),
-            jax.ShapeDtypeStruct((256, 512), jnp.bfloat16),
-            jax.ShapeDtypeStruct((128, 128), jnp.bfloat16),
-            (8, 128),
-            (8, 128),
             (128, 144),
-            (144, 128),
             (200, 16),
-            (16, 192),
         ],
         (
             flow_state,
@@ -849,24 +944,33 @@
             coordinates,
             face_neighbour,
             element_nodes,
-            sends_row,
-            flags_row,
-            damping_row,
-            jnp.asarray(constant_tables()),
+            held_tables,
         ),
         pl.CostEstimate(flops=200_000_000, bytes_accessed=1_000_000, transcendentals=100_000),
     )
-    residual, table, send_a, send_b, spans, outer, slopes = call(
-        main_kernel,
-        [
-            (5, 64, 64),
-            (8, 256),
-            (8, 128),
-            (8, 128),
-            (200, 384),
-            (5, 48, 128),
-            (3, 48, 128),
-        ],
+    group = min(16, count)
+    near = [[base + g for g in range(group)] for base in range(0, count, group)]
+    far = [[base + group * g for g in range(count // group)] for base in range(group)]
+    descent, sums = call(
+        core_kernel,
+        [(3, 128), (group, 1, 128)],
+        (
+            got_a,
+            got_b,
+            got_c,
+            got_d,
+            up,
+            down,
+            flagged,
+            sends,
+            held_tables,
+            held_damping,
+        ),
+        scratch=(pltpu.VMEM((5, 64, 128), F32),),
+    )
+    residual, change = call(
+        plane_kernel,
+        [(5, 64, 64)] * 2,
         (
             inner,
             state,
@@ -874,48 +978,12 @@
             places,
             border,
             node_index,
-            send_index,
-            named,
-            weight,
-            smoothing,
             got_a,
             got_b,
             assemble,
-            transposed,
             corner,
-            corner_transposed,
         ),
-    )
-    back_a, back_b = exchange(send_a, send_b, count)
-    change, token = call(
-        change_kernel,
-        [(5, 64, 64), (8, 128)],
-        (inner, state, local, border, got_a, got_b, assemble, spans, outer),
         pl.CostEstimate(flops=200_000_000, bytes_accessed=1_000_000, transcendentals=100_000),
-    )
-    group = min(16, count)
-    near = [[base + g for g in range(group)] for base in range(0, count, group)]
-    far = [[base + group * g for g in range(count // group)] for base in range(group)]
-    descent, sums = call(
-        second_kernel,
-        [(3, 128), (group, 1, 128)],
-        (
-            inner,
-            state,
-            node_index,
-            chosen,
-            weight,
-            smoothing,
-            table,
-            back_a,
-            back_b,
-            spans,
-            outer,
-            slopes,
-            assemble,
-            corner,
-            token,
-        ),
     )
     sums = lax.all_to_all(sums, "parts", 0, 0, axis_index_groups=near)
     if count > group:

time: 67.2 us -> 63 us (0.938)
  blocking collectives: 30.5 us -> 16.6 us
  starting transfers between devices: 22.3 us -> 28.3 us
  waiting for transfers between devices: 2.52 us -> 6.89 us
  local copies, waits for them, and re-layouts: 1.69 us -> 0.64 us
    all_to_all x1 -> x0, blocking collectives: 15.6 us -> none  [step(): sums = lax.all_to_all(sums, 'parts', 0, 0, axis_index_groups=far)]
    all_to_all x0 -> x1, waiting for transfers between devices: none -> 5.74 us  [step(): sums = lax.all_to_all(sums, 'parts', 0, 0, axis_index_groups=far)]
    all_to_all x0 -> x1, starting transfers between devices: none -> 3.92 us  [step(): sums = lax.all_to_all(sums, 'parts', 0, 0, axis_index_groups=far)]
    ppermute x4, starting transfers between devices: 22.3 us -> 24.3 us  [swapped(): return lax.ppermute(value, 'parts', [(i, partner(i)) for i in range(count)])]
    unnamed x20 -> x12, local copies, waits for them, and re-layouts: 1.68 us -> 0.02 us
    all_to_all x1, blocking collectives: 14.9 us -> 16.6 us  [step(): sums = lax.all_to_all(sums, 'parts', 0, 0, axis_index_groups=near)]
    ppermute x4, waiting for transfers between devices: 2.52 us -> 1.15 us  [swapped(): return lax.ppermute(value, 'parts', [(i, partner(i)) for i in range(count)])]
    pallas_call x6 -> x5, Pallas kernels: 8.91 us -> 9.5 us  [call(): pl.pallas_call(kernel, out_shape=[s if isinstance(s, jax.ShapeDtypeStruct...]
  transfers between devices with their start and end apart: 4 -> 5, of which waited for: 2 -> 2; matrix products, arithmetic and copies ran while one was open for 0% -> 0% of each run, Pallas kernels for 3% -> 5%
where the time goes in v2:
time: 63 us; the launch traced here: 62.6 us
  starting transfers between devices  28.3 us (45%)
  blocking collectives  16.6 us (26%)
  Pallas kernels  9.5 us (15%)
  waiting for transfers between devices  6.89 us (11%)
  between operations  0.76 us (1%)
  local copies, waits for them, and re-layouts  0.64 us (1%)
    ppermute x4, starting transfers between devices, swapped(): return lax.ppermute(value, 'parts', [(i, partner(i)) for i in range(count)])  24.3 us
    all_to_all x1, blocking collectives, step(): sums = lax.all_to_all(sums, 'parts', 0, 0, axis_index_groups=near)  16.6 us
    pallas_call x5, Pallas kernels, call(): pl.pallas_call(kernel, out_shape=[s if isinstance(s, jax.ShapeDtypeStruct...  9.5 us
    all_to_all x1, waiting for transfers between devices, step(): sums = lax.all_to_all(sums, 'parts', 0, 0, axis_index_groups=far)  5.74 us
    all_to_all x1, starting transfers between devices, step(): sums = lax.all_to_all(sums, 'parts', 0, 0, axis_index_groups=far)  3.92 us
  transfers between devices with their start and end apart: 5, of which 2 were waited for; matrix products, arithmetic and copies ran while one was open for 0% of the time, Pallas kernels for 5%

profile of v2, /device:TPU:1, one launch (start us, length us, event | category | flops | bytes accessed | tf_op | source)
XLA Modules:
  0.0 62.6 jit_solution(16987402700727287356)
XLA Ops:
  0.6 1.8 %shard_map.139 = (f32[184,128]{1,0:T(8,128)S(1)}, f32[184,128]{1,0:T(8,128)S(1)}, f32[40,128]{1,0:T(8,128)S(1)}, f32[40,128]{1,0:T(8,128)S(1)}, f32[56,128]{1,0:...) custom-call(f32[5,64,64]{2,1,0:T(8,128)} %flow_ref.1, ...), custom_call_target="tpu_custom_call" | custom-call | tf_op jit(solution)/shard_map/pallas_call | solution.py:829
  2.4 8.7 %collective-permute-start = (f32[184,128]{1,0:T(8,128)S(1)}, f32[184,128]{1,0:T(8,128)S(1)}, u32[]{:S(2)}, u32[]{:S(2)}) collective-permute-start(f32[184,128]{1,0:T(8,128)S(1)} %get-tuple-element.32), channel_id=1, source_target_pairs={{0,1},{1,0},{2,3},{3,2},{4,5},{5,4},{6,7},{7,6},{8,9},{9,8},{10,11... | collective-permute-start | bytes 282632 | tf_op jit(solution)/shard_map/ppermute | solution.py:853
  11.2 1.9 %collective-permute-start.1 = (f32[184,128]{1,0:T(8,128)S(1)}, f32[184,128]{1,0:T(8,128)S(1)}, u32[]{:S(2)}, u32[]{:S(2)}) collective-permute-start(f32[184,128]{1,0:T(8,128)S(1)} %get-tuple-element.33), channel_id=1, source_target_pairs={{0,511},{1,2},{2,1},{3,4},{4,3},{5,6},{6,5},{7,8},{8,7},{9,10},{10... | collective-permute-start | bytes 282632 | tf_op jit(solution)/shard_map/ppermute | solution.py:853
  13.1 1.9 %collective-permute-start.2 = (f32[40,128]{1,0:T(8,128)S(1)}, f32[40,128]{1,0:T(8,128)S(1)}, u32[]{:S(2)}, u32[]{:S(2)}) collective-permute-start(f32[40,128]{1,0:T(8,128)S(1)} %get-tuple-element.38), channel_id=1, source_target_pairs={{0,2},{1,3},{2,0},{3,1},{4,6},{5,7},{6,4},{7,5},{8,10},{9,11},{10,... | collective-permute-start | bytes 61448 | tf_op jit(solution)/shard_map/ppermute | solution.py:853
  15.1 11.8 %collective-permute-start.3 = (f32[40,128]{1,0:T(8,128)S(1)}, f32[40,128]{1,0:T(8,128)S(1)}, u32[]{:S(2)}, u32[]{:S(2)}) collective-permute-start(f32[40,128]{1,0:T(8,128)S(1)} %get-tuple-element.39), channel_id=1, source_target_pairs={{0,510},{1,511},{2,4},{3,5},{4,2},{5,3},{6,8},{7,9},{8,6},{9,7},{1... | collective-permute-start | bytes 61448 | tf_op jit(solution)/shard_map/ppermute | solution.py:853
  26.8 0.0 collective-permute-done.2.c_ref
  26.8 1.1 %collective-permute-done.3.d_ref = f32[40,128]{1,0:T(8,128)S(1)} collective-permute-done((f32[40,128]{1,0:T(8,128)S(1)}, f32[40,128]{1,0:T(8,128)S(1)}, u32[]{:S(2)}, u32[]{:S(2)}) %collective-permute-start.3) | collective-permute-done | bytes 20512 | tf_op jit(solution)/shard_map/ppermute | solution.py:853
  28.0 0.0 collective-permute-done.a_ref
  28.0 0.0 collective-permute-done.1.b_ref
  28.0 0.0 copy-start.1
  28.0 4.1 %shard_map.142 = (f32[3,128]{1,0:T(4,128)S(1)}, f32[16,1,128]{2,1,0:T(1,128)S(1)}) custom-call(f32[184,128]{1,0:T(8,128)S(1)} %collective-permute-done.a_ref, f32[184,128]{1,0:T(8,128)S(1)} %collective-permute-done.1.b_ref, f32[40,128]{1,0:T(8,128)S(1)} %collective-permute-done.2.c_ref, f32[40,128]{1,0:T(8,128)S(1)} %collective-permute-done.3.d_ref, ...), custom_call_target="tpu_custom_call" | custom-call | tf_op jit(solution)/shard_map/pallas_call | solution.py:829
  32.1 16.6 %all_to_all.10 = f32[16,1,128]{2,1,0:T(1,128)S(1)} all-to-all(f32[16,1,128]{2,1,0:T(1,128)S(1)} %get-tuple-element.45), channel_id=1, replica_groups={{0,1,2,3,4,5,6,7,8,9,10,11,12,13,14,15},{16,17,18,19,20,21,22,23,24,25,..., dimensions={0} | all-to-all | bytes 16384 | tf_op jit(solution)/shard_map/all_to_all | solution.py:988
  48.7 0.6 broadcast_in_dim.2
  49.3 3.9 %all-to-all-start.1 = ((f32[32,1,128]{2,1,0:T(1,128)}), f32[32,1,128]{2,1,0:T(1,128)S(1)}, u32[]{:S(2)}, u32[]{:S(2)}) async-start(f32[32,1,128]{2,1,0:T(1,128)} %broadcast_in_dim.2), calls=%async_computation.1 | async-start | bytes 32768 | tf_op jit(solution)/shard_map/all_to_all | solution.py:991
  53.3 0.0 copy-done
  53.3 0.0 copy-done.1
  53.3 0.0 copy-done.2
  53.3 0.0 copy-done.3
  53.3 0.0 copy-done.4
  53.3 0.0 copy-done.5
  53.3 0.6 shard_map.140
  53.9 2.3 %shard_map.141 = (f32[5,64,64]{2,1,0:T(8,128)}, f32[5,64,64]{2,1,0:T(8,128)}) custom-call(f32[10,48,128]{2,1,0:T(8,128)S(1)} %get-tuple-element.26.inner_ref, f32[10,32,128]{2,1,0:T(8,128)S(1)} %get-tuple-element.27.state_ref, f32[10,48,128]{2,1,0:T(8,128)S(1)} %get-tuple-element.28.local_ref, f32[8,128]{1,0:T(8,128)S(1)} %get-tuple-element.29.places_ref, ...), custom_call_target="tpu_custom_call" | custom-call | flops 200000000 | bytes 1000000 | tf_op jit(solution)/shard_map/pallas_call | solution.py:829
  56.2 5.7 %all-to-all-done.1.sums_ref = f32[32,1,128]{2,1,0:T(1,128)S(1)} async-done(((f32[32,1,128]{2,1,0:T(1,128)}), f32[32,1,128]{2,1,0:T(1,128)S(1)}, u32[]{:S(2)}, u32[]{:S(2)}) %all-to-all-start.1) | async-done | bytes 16416 | tf_op jit(solution)/shard_map/all_to_all | solution.py:991
  61.9 0.7 %shard_map.143 = f32[3,102]{1,0:T(4,128)} custom-call(f32[32,1,128]{2,1,0:T(1,128)S(1)} %all-to-all-done.1.sums_ref, f32[3,128]{1,0:T(4,128)S(1)} %get-tuple-element.46.descent_ref), custom_call_target="tpu_custom_call" | custom-call | tf_op jit(solution)/shard_map/pallas_call | solution.py:829
  (6 shorter events, 0.0 us)
Async XLA Ops:
  2.4 25.5 %collective-permute-start = (f32[184,128]{1,0:T(8,128)S(1)}, f32[184,128]{1,0:T(8,128)S(1)}, u32[]{:S(2)}, u32[]{:S(2)}) collective-permute-start(f32[184,128]{1,0:T(8,128)S(1)} %get-tuple-element.32), channel_id=1, source_target_pairs={{0,1},{1,0},{2,3},{3,2},{4,5},{5,4},{6,7},{7,6},{8,9},{9,8},{10,11... | collective-permute-start | bytes 282632 | tf_op jit(solution)/shard_map/ppermute | solution.py:853
  11.2 16.8 %collective-permute-start.1 = (f32[184,128]{1,0:T(8,128)S(1)}, f32[184,128]{1,0:T(8,128)S(1)}, u32[]{:S(2)}, u32[]{:S(2)}) collective-permute-start(f32[184,128]{1,0:T(8,128)S(1)} %get-tuple-element.33), channel_id=1, source_target_pairs={{0,511},{1,2},{2,1},{3,4},{4,3},{5,6},{6,5},{7,8},{8,7},{9,10},{10... | collective-permute-start | bytes 282632 | tf_op jit(solution)/shard_map/ppermute | solution.py:853
  13.1 13.7 %collective-permute-start.2 = (f32[40,128]{1,0:T(8,128)S(1)}, f32[40,128]{1,0:T(8,128)S(1)}, u32[]{:S(2)}, u32[]{:S(2)}) collective-permute-start(f32[40,128]{1,0:T(8,128)S(1)} %get-tuple-element.38), channel_id=1, source_target_pairs={{0,2},{1,3},{2,0},{3,1},{4,6},{5,7},{6,4},{7,5},{8,10},{9,11},{10,... | collective-permute-start | bytes 61448 | tf_op jit(solution)/shard_map/ppermute | solution.py:853
  15.1 12.9 %collective-permute-start.3 = (f32[40,128]{1,0:T(8,128)S(1)}, f32[40,128]{1,0:T(8,128)S(1)}, u32[]{:S(2)}, u32[]{:S(2)}) collective-permute-start(f32[40,128]{1,0:T(8,128)S(1)} %get-tuple-element.39), channel_id=1, source_target_pairs={{0,510},{1,511},{2,4},{3,5},{4,2},{5,3},{6,8},{7,9},{8,6},{9,7},{1... | collective-permute-start | bytes 61448 | tf_op jit(solution)/shard_map/ppermute | solution.py:853
  28.0 25.3 %copy-start = (f32[5,64,64]{2,1,0:T(8,128)S(1)}, f32[5,64,64]{2,1,0:T(8,128)}, u32[]{:S(2)}) copy-start(f32[5,64,64]{2,1,0:T(8,128)} %flow_ref.1) | copy-start | bytes 245764
  28.0 25.3 %copy-start.1 = (f32[5,64,64]{2,1,0:T(8,128)S(1)}, f32[5,64,64]{2,1,0:T(8,128)}, u32[]{:S(2)}) copy-start(f32[5,64,64]{2,1,0:T(8,128)} %tangent_ref.1) | copy-start | bytes 245764
  49.3 4.0 %copy-start.2 = (s32[6,64]{1,0:T(8,128)S(1)}, s32[6,64]{1,0:T(8,128)}, u32[]{:S(2)}) copy-start(s32[6,64]{1,0:T(8,128)} %neighbour_ref.1) | copy-start | bytes 4612
  49.3 4.0 %copy-start.3 = (s32[8,64]{1,0:T(8,128)S(1)}, s32[8,64]{1,0:T(8,128)}, u32[]{:S(2)}) copy-start(s32[8,64]{1,0:T(8,128)} %nodes_ref.1) | copy-start | bytes 6148
  49.3 4.0 %copy-start.4 = (f32[3,102]{1,0:T(4,128)S(1)}, f32[3,102]{1,0:T(4,128)}, u32[]{:S(2)}) copy-start(f32[3,102]{1,0:T(4,128)} %places_ref.1) | copy-start | bytes 3676
  49.3 4.0 %copy-start.5 = (f32[5]{0:T(128)S(1)}, f32[5]{0:T(128)}, u32[]{:S(2)}) copy-start(f32[5]{0:T(128)} %param.14) | copy-start | bytes 64
  49.3 12.6 %all-to-all-start.1 = ((f32[32,1,128]{2,1,0:T(1,128)}), f32[32,1,128]{2,1,0:T(1,128)S(1)}, u32[]{:S(2)}, u32[]{:S(2)}) async-start(f32[32,1,128]{2,1,0:T(1,128)} %broadcast_in_dim.2), calls=%async_computation.1 | async-start | bytes 32768 | tf_op jit(solution)/shard_map/all_to_all | solution.py:991

commit v3 on v2

--- a/solution.py
+++ b/solution.py
@@ -258,15 +258,12 @@
         b_ref,
         c_ref,
         d_ref,
-        up_ref,
-        down_ref,
-        flagged_ref,
         sends_out,
         tables_out,
         damping_out,
-    ) = refs[12:22]
-    held = refs[22:32]
-    semaphores = refs[32]
+    ) = refs[12:19]
+    held = refs[19:29]
+    semaphores = refs[29]
     moves = list(zip(sources, held)) + [(tables_hbm, tables_out), (damping_hbm, damping_out)]
     copies = [
         pltpu.make_async_copy(source, target, semaphores.at[i])
@@ -318,8 +315,8 @@
     row8 = lax.broadcasted_iota(jnp.int32, (8, 128), 0)
     nodes = jnp.where(row8 == 3, spread(sends_row.astype(F32)), nodes)
     none = jnp.zeros((8, 128), F32)
-    up = jnp.concatenate([up, none], axis=0)
-    down = jnp.concatenate([down, nodes], axis=0)
+    spare = jnp.where(lane >= 64, pltpu.roll(nodes, 64, 1), down[32:40])
+    down = jnp.concatenate([down[0:32], spare, down[40:48]], axis=0)
 
     flags = pad_lanes(flags_ref[...].astype(F32))
     first_row = lax.broadcasted_iota(jnp.int32, (64, 128), 0)
@@ -359,20 +356,26 @@
         packed.append(
             merged_blocks([pick(value[8 * b : 8 * b + 8], chosen) for b in range(8)])
         )
+    inner = [face_pairs(flow_ref, v) for v in range(5)]
+
+    def beside_part(v, chunk, side):
+        far, local = beside[chunk // 2][side]
+        taken = pick(inner[v][8 * chunk : 8 * chunk + 8], local)
+        return jnp.where(far, far_ref[0:1, v : v + 1], taken)
+
     for v in range(5):
-        inner = face_pairs(flow_ref, v)
-        far_value = far_ref[0:1, v : v + 1]
-        for first in (0, 4):
-            parts = []
-            for b in range(8):
-                chunk, side = first + b % 4, b // 4
-                if chunk >= 6:
-                    parts.append(none)
-                    continue
-                far, local = beside[chunk // 2][side]
-                taken = pick(inner[8 * chunk : 8 * chunk + 8], local)
-                parts.append(jnp.where(far, far_value, taken))
-            packed.append(merged_blocks(parts))
+        packed.append(merged_blocks([beside_part(v, b % 4, b // 4) for b in range(8)]))
+    for first in (0, 2, 4):
+        packed.append(
+            merged_blocks(
+                [
+                    beside_part(first + b % 4 // 2, 4 + b % 2, b // 4)
+                    if first + b % 4 // 2 < 5
+                    else none
+                    for b in range(8)
+                ]
+            )
+        )
     node_index = pick(pair(nodes_ref[...], nodes_ref[...]), chosen)
     local_node = jnp.where(node_index < 102, node_index, 0)
     codes = jnp.where(
@@ -387,20 +390,15 @@
         )
     )
     flagged = jnp.concatenate(packed, axis=0)
-    flagged_ref[...] = flagged
     sends_out[...] = sends_ref[...]
-    up_ref[...] = up
-    down_ref[...] = down
     odd = position_bit(0)
     second = position_bit(1)
-    a_ref[0:56] = jnp.where(odd, down, up)
-    b_ref[0:56] = jnp.where(odd, up, down)
-    a_ref[56:184] = flagged
-    b_ref[56:184] = flagged
-    short_up = jnp.concatenate([up[0:32], up[48:56]], axis=0)
-    short_down = jnp.concatenate([down[0:32], down[48:56]], axis=0)
-    c_ref[...] = jnp.where(second, short_down, short_up)
-    d_ref[...] = jnp.where(second, short_up, short_down)
+    a_ref[0:48] = jnp.where(odd, down, up)
+    b_ref[0:48] = jnp.where(odd, up, down)
+    a_ref[48:160] = flagged
+    b_ref[48:160] = flagged
+    c_ref[...] = jnp.where(second, down, up)
+    d_ref[...] = jnp.where(second, up, down)
     for copy in copies[10:12]:
         copy.wait()
 
@@ -564,12 +562,12 @@
     change_ref,
 ):
     odd = position_bit(0)
-    from_a = a_ref[0:56]
-    from_b = b_ref[0:56]
-    lower = jnp.where(odd, from_a, from_b)
-    upper = jnp.where(odd, from_b, from_a)
+    lower = jnp.where(odd, a_ref[0:48], b_ref[0:48])
+    upper = jnp.where(odd, b_ref[0:48], a_ref[0:48])
     border = Border(border_ref[...], lower, upper)
-    corners = corner_values(node_index_ref[...], places_ref[...], upper[48:56])
+    corners = corner_values(
+        node_index_ref[...], places_ref[...], pltpu.roll(upper[32:40], 64, 1)
+    )
     spans = dot(corner_ref[...], corner_operand([c - c[0:1] for c in corners]))
     volume_spans, face_spans = tangents_of(spans)
     normals, face_normal, area_square, area = geometry(volume_spans, face_spans)
@@ -596,9 +594,8 @@
     b_ref,
     c_ref,
     d_ref,
-    up_ref,
-    down_ref,
-    flagged_ref,
+    sent_a_ref,
+    sent_b_ref,
     sends_ref,
     tables_ref,
     damping_ref,
@@ -612,9 +609,9 @@
     upper = jnp.where(odd, b_ref[...], a_ref[...])
     lower_two = jnp.where(second, c_ref[...], d_ref[...])
     upper_two = jnp.where(second, d_ref[...], c_ref[...])
-    up = up_ref[...]
-    down = down_ref[...]
-    flagged = flagged_ref[...]
+    up = jnp.where(odd, sent_b_ref[0:48], sent_a_ref[0:48])
+    down = jnp.where(odd, sent_a_ref[0:48], sent_b_ref[0:48])
+    flagged = sent_a_ref[48:160]
     lane = lanes()
     low = lane < 64
     seat = lane % 16
@@ -625,7 +622,7 @@
 
     def taken(row, index):
         rows = slice(row, row + 8)
-        moved = slice(56 + row, 64 + row)
+        moved = slice(48 + row, 56 + row)
         return three(
             pick(flagged[rows], index), pick(lower[moved], index), pick(upper[moved], index)
         )
@@ -646,7 +643,7 @@
             last = whole_ref[pl.ds(v, 1), pl.ds(3 * s, 16, stride=4), :][0]
             sides.append(jnp.concatenate([value[48 * s : 48 * s + 16], middle, last], axis=0))
         inner.append(jnp.where(lanes(48) < 64, sides[0], sides[1]))
-    codes = taken(120, seat + 64)
+    codes = taken(104, seat + 64)
     border = spread(jnp.where(low[0:1], codes[0:1], codes[1:2])).astype(jnp.int32)
     weight = jnp.where(block[0:1] == 3, 0.0, codes[2:3])
     slot = jnp.clip(border - 64, 0, 31)
@@ -655,8 +652,11 @@
     for v in range(5):
         chunks = []
         for chunk in range(6):
-            index = seat + 16 * (chunk % 4) + jnp.where(low, 0, 64)
-            value = taken(40 + 16 * v + 8 * (chunk // 4), index)
+            if chunk < 4:
+                row, place = 40 + 8 * v, chunk
+            else:
+                row, place = 80 + 8 * (v // 2), chunk - 4 + 2 * (v % 2)
+            value = taken(row, seat + 16 * place + jnp.where(low, 0, 64))
             if chunk < 2:
                 rows = slice(16 * (v // 4) + 8 * chunk, 16 * (v // 4) + 8 * chunk + 8)
                 at = slot + 32 * (v % 4)
@@ -667,16 +667,16 @@
                 value = jnp.where(halo, jnp.where(low, side0, side1), value)
             chunks.append(value)
         outer.append(jnp.concatenate(chunks, axis=0))
-    node_index = taken(120, seat + 48).astype(jnp.int32)
+    node_index = taken(104, seat + 48).astype(jnp.int32)
     foreign = node_index >= 102
     foreign_slot = jnp.where(foreign, node_index - 102, 0)
     corners = []
     for i in range(3):
-        local = taken(120, seat + 16 * i)
+        local = taken(104, seat + 16 * i)
         remote = three(
-            pick(spread(upper[48 + i : 49 + i]), foreign_slot),
-            pick(spread(down[48 + i : 49 + i]), foreign_slot),
-            pick(spread(upper_two[32 + i : 33 + i]), foreign_slot),
+            pick(spread(upper[32 + i : 33 + i]), foreign_slot + 64),
+            pick(spread(down[32 + i : 33 + i]), foreign_slot + 64),
+            pick(spread(upper_two[32 + i : 33 + i]), foreign_slot + 64),
         )
         corners.append(jnp.where(foreign, remote, local))
 
@@ -750,7 +750,9 @@
     halo_node = jnp.where(block == 0, jnp.where(foreign, node_index - 102, -1), nowhere)
     upper_node = jnp.where((block == 2) & ~foreign, node_index, -1)
     square_row = lax.broadcasted_iota(jnp.int32, (128, 128), 0)
-    upper_sends = jnp.where(lane[0:1] < 51, upper[51:52], -5.0)
+    upper_sends = jnp.where(
+        lane[0:1] < 51, pltpu.roll(spread(upper[35:36]), 64, 1)[0:1], -5.0
+    )
     upper_column = jnp.sum(
         jnp.where(square_row == lanes(128), jnp.broadcast_to(upper_sends, (128, 128)), 0.0),
         axis=1,
@@ -876,10 +878,11 @@
     damping_row = damping.reshape(1, 2)
     integer = jnp.int32
     tables = jnp.asarray(constant_tables())
-    pack_a, pack_b, pack_c, pack_d, up, down, flagged, sends, held_tables, held_damping = call(
+    pack_a, pack_b, pack_c, pack_d, sends, held_tables, held_damping = call(
         pack_kernel,
-        [(184, 128)] * 2 + [(40, 128)] * 2 + [(56, 128)] * 2
-        + [(128, 128), jax.ShapeDtypeStruct((1, 51), integer), (488, 256), (1, 2)],
+        [(160, 128)] * 2
+        + [(48, 128)] * 2
+        + [jax.ShapeDtypeStruct((1, 51), integer), (488, 256), (1, 2)],
         tuple(
             stays(x)
             for x in (
@@ -912,8 +915,8 @@
             pltpu.SemaphoreType.DMA((12,)),
         ),
     )
+    got_b = swapped(pack_b, lambda i: beyond(i, count))
     got_d = swapped(pack_d, lambda i: beyond_two(i, count))
-    got_b = swapped(pack_b, lambda i: beyond(i, count))
     got_c = swapped(pack_c, lambda i: i ^ 2)
     got_a = swapped(pack_a, lambda i: i ^ 1)
     (
@@ -959,9 +962,8 @@
             got_b,
             got_c,
             got_d,
-            up,
-            down,
-            flagged,
+            pack_a,
+            pack_b,
             sends,
             held_tables,
             held_damping,

time: 63 us -> 62.9 us (level)
  no operation moved by 1% of the time
where the time goes in v3:
time: 62.9 us; the launch traced here: 62.6 us
  starting transfers between devices  28.3 us (45%)
  blocking collectives  16.6 us (26%)
  Pallas kernels  9.48 us (15%)
  waiting for transfers between devices  6.85 us (11%)
  between operations  0.76 us (1%)
  local copies, waits for them, and re-layouts  0.64 us (1%)
    ppermute x4, starting transfers between devices, swapped(): return lax.ppermute(value, 'parts', [(i, partner(i)) for i in range(count)])  24.3 us
    all_to_all x1, blocking collectives, step(): sums = lax.all_to_all(sums, 'parts', 0, 0, axis_index_groups=near)  16.6 us
    pallas_call x5, Pallas kernels, call(): pl.pallas_call(kernel, out_shape=[s if isinstance(s, jax.ShapeDtypeStruct...  9.48 us
    all_to_all x1, waiting for transfers between devices, step(): sums = lax.all_to_all(sums, 'parts', 0, 0, axis_index_groups=far)  5.65 us
    all_to_all x1, starting transfers between devices, step(): sums = lax.all_to_all(sums, 'parts', 0, 0, axis_index_groups=far)  3.92 us
  transfers between devices with their start and end apart: 5, of which 2 were waited for; matrix products, arithmetic and copies ran while one was open for 0% of the time, Pallas kernels for 5%

profile of v3, /device:TPU:1, one launch (start us, length us, event | category | flops | bytes accessed | tf_op | source)
XLA Modules:
  0.0 62.6 jit_solution(16772593383785134311)
XLA Ops:
  0.6 1.7 %shard_map.139 = (f32[160,128]{1,0:T(8,128)S(1)}, f32[160,128]{1,0:T(8,128)S(1)}, f32[48,128]{1,0:T(8,128)S(1)}, f32[48,128]{1,0:T(8,128)S(1)}, s32[1,51]{1,0:T(...) custom-call(f32[5,64,64]{2,1,0:T(8,128)} %flow_ref.1, f32[5,64,64]{2,1,0:T(8,128)} %tangent_ref.1, ...), custom_call_target="tpu_custom_call" | custom-call | tf_op jit(solution)/shard_map/pallas_call | solution.py:831
  2.3 8.7 %collective-permute-start = (f32[160,128]{1,0:T(8,128)S(1)}, f32[160,128]{1,0:T(8,128)S(1)}, u32[]{:S(2)}, u32[]{:S(2)}) collective-permute-start(f32[160,128]{1,0:T(8,128)S(1)} %get-tuple-element.29.sent_a_ref), channel_id=1, source_target_pairs={{0,1},{1,0},{2,3},{3,2},{4,5},{5,4},{6,7},{7,6},{8,9},{9,8},{10,11... | collective-permute-start | bytes 245768 | tf_op jit(solution)/shard_map/ppermute | solution.py:855
  11.1 1.9 %collective-permute-start.1 = (f32[160,128]{1,0:T(8,128)S(1)}, f32[160,128]{1,0:T(8,128)S(1)}, u32[]{:S(2)}, u32[]{:S(2)}) collective-permute-start(f32[160,128]{1,0:T(8,128)S(1)} %get-tuple-element.30.sent_b_ref), channel_id=1, source_target_pairs={{0,511},{1,2},{2,1},{3,4},{4,3},{5,6},{6,5},{7,8},{8,7},{9,10},{10... | collective-permute-start | bytes 245768 | tf_op jit(solution)/shard_map/ppermute | solution.py:855
  13.0 1.9 %collective-permute-start.2 = (f32[48,128]{1,0:T(8,128)S(1)}, f32[48,128]{1,0:T(8,128)S(1)}, u32[]{:S(2)}, u32[]{:S(2)}) collective-permute-start(f32[48,128]{1,0:T(8,128)S(1)} %get-tuple-element.35), channel_id=1, source_target_pairs={{0,2},{1,3},{2,0},{3,1},{4,6},{5,7},{6,4},{7,5},{8,10},{9,11},{10,... | collective-permute-start | bytes 73736 | tf_op jit(solution)/shard_map/ppermute | solution.py:855
  15.0 11.8 %collective-permute-start.3 = (f32[48,128]{1,0:T(8,128)S(1)}, f32[48,128]{1,0:T(8,128)S(1)}, u32[]{:S(2)}, u32[]{:S(2)}) collective-permute-start(f32[48,128]{1,0:T(8,128)S(1)} %get-tuple-element.36), channel_id=1, source_target_pairs={{0,510},{1,511},{2,4},{3,5},{4,2},{5,3},{6,8},{7,9},{8,6},{9,7},{1... | collective-permute-start | bytes 73736 | tf_op jit(solution)/shard_map/ppermute | solution.py:855
  26.7 0.0 collective-permute-done.2.c_ref
  26.7 1.2 %collective-permute-done.3.d_ref = f32[48,128]{1,0:T(8,128)S(1)} collective-permute-done((f32[48,128]{1,0:T(8,128)S(1)}, f32[48,128]{1,0:T(8,128)S(1)}, u32[]{:S(2)}, u32[]{:S(2)}) %collective-permute-start.3) | collective-permute-done | bytes 24608 | tf_op jit(solution)/shard_map/ppermute | solution.py:855
  27.9 0.0 collective-permute-done.a_ref
  27.9 0.0 collective-permute-done.1.b_ref
  27.9 0.0 copy-start.1
  27.9 4.1 %shard_map.142 = (f32[3,128]{1,0:T(4,128)S(1)}, f32[16,1,128]{2,1,0:T(1,128)S(1)}) custom-call(f32[160,128]{1,0:T(8,128)S(1)} %collective-permute-done.a_ref, f32[160,128]{1,0:T(8,128)S(1)} %collective-permute-done.1.b_ref, f32[48,128]{1,0:T(8,128)S(1)} %collective-permute-done.2.c_ref, f32[48,128]{1,0:T(8,128)S(1)} %collective-permute-done.3.d_ref, ...), custom_call_target="tpu_custom_call" | custom-call | tf_op jit(solution)/shard_map/pallas_call | solution.py:831
  32.0 16.6 %all_to_all.10 = f32[16,1,128]{2,1,0:T(1,128)S(1)} all-to-all(f32[16,1,128]{2,1,0:T(1,128)S(1)} %get-tuple-element.39), channel_id=1, replica_groups={{0,1,2,3,4,5,6,7,8,9,10,11,12,13,14,15},{16,17,18,19,20,21,22,23,24,25,..., dimensions={0} | all-to-all | bytes 16384 | tf_op jit(solution)/shard_map/all_to_all | solution.py:990
  48.6 0.6 broadcast_in_dim.2
  49.3 3.9 %all-to-all-start.1 = ((f32[32,1,128]{2,1,0:T(1,128)}), f32[32,1,128]{2,1,0:T(1,128)S(1)}, u32[]{:S(2)}, u32[]{:S(2)}) async-start(f32[32,1,128]{2,1,0:T(1,128)} %broadcast_in_dim.2), calls=%async_computation.1 | async-start | bytes 32768 | tf_op jit(solution)/shard_map/all_to_all | solution.py:993
  53.2 0.0 copy-done
  53.2 0.0 copy-done.1
  53.2 0.0 copy-done.2
  53.2 0.0 copy-done.3
  53.2 0.0 copy-done.4
  53.2 0.0 copy-done.5
  53.2 0.6 shard_map.140
  53.8 2.4 %shard_map.141 = (f32[5,64,64]{2,1,0:T(8,128)}, f32[5,64,64]{2,1,0:T(8,128)}) custom-call(f32[10,48,128]{2,1,0:T(8,128)S(1)} %get-tuple-element.23.inner_ref, f32[10,32,128]{2,1,0:T(8,128)S(1)} %get-tuple-element.24.state_ref, f32[10,48,128]{2,1,0:T(8,128)S(1)} %get-tuple-element.25.local_ref, f32[8,128]{1,0:T(8,128)S(1)} %get-tuple-element.26.places_ref, ...), custom_call_target="tpu_custom_call" | custom-call | flops 200000000 | bytes 1000000 | tf_op jit(solution)/shard_map/pallas_call | solution.py:831
  56.2 5.6 %all-to-all-done.1.sums_ref = f32[32,1,128]{2,1,0:T(1,128)S(1)} async-done(((f32[32,1,128]{2,1,0:T(1,128)}), f32[32,1,128]{2,1,0:T(1,128)S(1)}, u32[]{:S(2)}, u32[]{:S(2)}) %all-to-all-start.1) | async-done | bytes 16416 | tf_op jit(solution)/shard_map/all_to_all | solution.py:993
  61.9 0.7 %shard_map.143 = f32[3,102]{1,0:T(4,128)} custom-call(f32[32,1,128]{2,1,0:T(1,128)S(1)} %all-to-all-done.1.sums_ref, f32[3,128]{1,0:T(4,128)S(1)} %get-tuple-element.40.descent_ref), custom_call_target="tpu_custom_call" | custom-call | tf_op jit(solution)/shard_map/pallas_call | solution.py:831
  (6 shorter events, 0.0 us)
Async XLA Ops:
  2.3 25.6 %collective-permute-start = (f32[160,128]{1,0:T(8,128)S(1)}, f32[160,128]{1,0:T(8,128)S(1)}, u32[]{:S(2)}, u32[]{:S(2)}) collective-permute-start(f32[160,128]{1,0:T(8,128)S(1)} %get-tuple-element.29.sent_a_ref), channel_id=1, source_target_pairs={{0,1},{1,0},{2,3},{3,2},{4,5},{5,4},{6,7},{7,6},{8,9},{9,8},{10,11... | collective-permute-start | bytes 245768 | tf_op jit(solution)/shard_map/ppermute | solution.py:855
  11.1 16.8 %collective-permute-start.1 = (f32[160,128]{1,0:T(8,128)S(1)}, f32[160,128]{1,0:T(8,128)S(1)}, u32[]{:S(2)}, u32[]{:S(2)}) collective-permute-start(f32[160,128]{1,0:T(8,128)S(1)} %get-tuple-element.30.sent_b_ref), channel_id=1, source_target_pairs={{0,511},{1,2},{2,1},{3,4},{4,3},{5,6},{6,5},{7,8},{8,7},{9,10},{10... | collective-permute-start | bytes 245768 | tf_op jit(solution)/shard_map/ppermute | solution.py:855
  13.0 13.7 %collective-permute-start.2 = (f32[48,128]{1,0:T(8,128)S(1)}, f32[48,128]{1,0:T(8,128)S(1)}, u32[]{:S(2)}, u32[]{:S(2)}) collective-permute-start(f32[48,128]{1,0:T(8,128)S(1)} %get-tuple-element.35), channel_id=1, source_target_pairs={{0,2},{1,3},{2,0},{3,1},{4,6},{5,7},{6,4},{7,5},{8,10},{9,11},{10,... | collective-permute-start | bytes 73736 | tf_op jit(solution)/shard_map/ppermute | solution.py:855
  15.0 13.0 %collective-permute-start.3 = (f32[48,128]{1,0:T(8,128)S(1)}, f32[48,128]{1,0:T(8,128)S(1)}, u32[]{:S(2)}, u32[]{:S(2)}) collective-permute-start(f32[48,128]{1,0:T(8,128)S(1)} %get-tuple-element.36), channel_id=1, source_target_pairs={{0,510},{1,511},{2,4},{3,5},{4,2},{5,3},{6,8},{7,9},{8,6},{9,7},{1... | collective-permute-start | bytes 73736 | tf_op jit(solution)/shard_map/ppermute | solution.py:855
  27.9 25.3 %copy-start = (f32[5,64,64]{2,1,0:T(8,128)S(1)}, f32[5,64,64]{2,1,0:T(8,128)}, u32[]{:S(2)}) copy-start(f32[5,64,64]{2,1,0:T(8,128)} %flow_ref.1) | copy-start | bytes 245764
  27.9 25.3 %copy-start.1 = (f32[5,64,64]{2,1,0:T(8,128)S(1)}, f32[5,64,64]{2,1,0:T(8,128)}, u32[]{:S(2)}) copy-start(f32[5,64,64]{2,1,0:T(8,128)} %tangent_ref.1) | copy-start | bytes 245764
  49.2 4.0 %copy-start.2 = (s32[6,64]{1,0:T(8,128)S(1)}, s32[6,64]{1,0:T(8,128)}, u32[]{:S(2)}) copy-start(s32[6,64]{1,0:T(8,128)} %neighbour_ref.1) | copy-start | bytes 4612
  49.3 4.0 %copy-start.3 = (s32[8,64]{1,0:T(8,128)S(1)}, s32[8,64]{1,0:T(8,128)}, u32[]{:S(2)}) copy-start(s32[8,64]{1,0:T(8,128)} %nodes_ref.1) | copy-start | bytes 6148
  49.3 4.0 %copy-start.4 = (f32[3,102]{1,0:T(4,128)S(1)}, f32[3,102]{1,0:T(4,128)}, u32[]{:S(2)}) copy-start(f32[3,102]{1,0:T(4,128)} %places_ref.1) | copy-start | bytes 3676
  49.3 4.0 %copy-start.5 = (f32[5]{0:T(128)S(1)}, f32[5]{0:T(128)}, u32[]{:S(2)}) copy-start(f32[5]{0:T(128)} %param.14) | copy-start | bytes 64
  49.3 12.6 %all-to-all-start.1 = ((f32[32,1,128]{2,1,0:T(1,128)}), f32[32,1,128]{2,1,0:T(1,128)S(1)}, u32[]{:S(2)}, u32[]{:S(2)}) async-start(f32[32,1,128]{2,1,0:T(1,128)} %broadcast_in_dim.2), calls=%async_computation.1 | async-start | bytes 32768 | tf_op jit(solution)/shard_map/all_to_all | solution.py:993

commit v4 on v3

--- a/solution.py
+++ b/solution.py
@@ -12,6 +12,7 @@
 GAMMA = 1.4
 SOFTENING = 0.01
 HIGHEST = lax.Precision.HIGHEST
+HIGH = lax.Precision.HIGH
 F32 = jnp.float32
 
 
@@ -111,8 +112,8 @@
     return tables
 
 
-def dot(a, b):
-    return jnp.dot(a, b, precision=HIGHEST, preferred_element_type=F32)
+def dot(a, b, precision=HIGHEST):
+    return jnp.dot(a, b, precision=precision, preferred_element_type=F32)
 
 
 def placed(a, chosen):
@@ -538,12 +539,12 @@
     return [along_flux(prims, normals[j]) for j in range(3)]
 
 
-def assembled(assemble, fluxes, jump):
+def assembled(assemble, fluxes, jump, precision=HIGHEST):
     stacked = [
         jnp.concatenate([fluxes[0][v], fluxes[1][v], fluxes[2][v], jump[v]], axis=0)
         for v in range(5)
     ]
-    product = dot(assemble, jnp.concatenate(stacked, axis=1))
+    product = dot(assemble, jnp.concatenate(stacked, axis=1), precision)
     return [folded(product, v) for v in range(5)]
 
 
@@ -696,7 +697,7 @@
                 axis=0,
             )
         )
-    back = dot(tables_ref[128:272, 0:128], jnp.concatenate(seeds, axis=1))
+    back = dot(tables_ref[128:272, 0:128], jnp.concatenate(seeds, axis=1), HIGH)
     prims = primitives(state)
     normal_bar = []
     for j in range(3):
@@ -728,7 +729,7 @@
         ],
         axis=1,
     )
-    corner_bar = dot(tables_ref[472:488, 0:192], stacked_bar)
+    corner_bar = dot(tables_ref[472:488, 0:192], stacked_bar, HIGH)
     smoothing = damping_ref[0:1, 1:2]
     pieces = []
     for i in range(3):
@@ -785,7 +786,7 @@
     norm = jnp.sum(moved * moved, axis=(0, 1), keepdims=True)
 
     steps = corner_values(node_index, own, halo_table)
-    moves = dot(tables_ref[272:472, 0:16], corner_operand(steps))
+    moves = dot(tables_ref[272:472, 0:16], corner_operand(steps), HIGH)
     volume_moves, face_moves = tangents_of(moves)
     fluxes = []
     for j in range(3):
@@ -805,7 +806,7 @@
         0.5 * (outer_flux[v] - inner_flux[v] - wave_move * (outer[v] - inner[v]))
         for v in range(5)
     ]
-    square = sum(change * change for change in assembled(tables_ref[0:128, 0:144], fluxes, jump))
+    square = sum(change * change for change in assembled(tables_ref[0:128, 0:144], fluxes, jump, HIGH))
     own_weight = jnp.where(lane[0:1] < 16, weight, 0.0)
     curvature = jnp.sum(
         jnp.sum(square, axis=0, keepdims=True) * own_weight, axis=1, keepdims=True

time: 62.9 us -> 62.3 us (level)
  no operation moved by 1% of the time
where the time goes in v4:
time: 62.3 us; the launch traced here: 62 us
  starting transfers between devices  28.3 us (45%)
  blocking collectives  16.5 us (26%)
  Pallas kernels  8.86 us (14%)
  waiting for transfers between devices  6.85 us (11%)
  between operations  0.76 us (1%)
  local copies, waits for them, and re-layouts  0.64 us (1%)
    ppermute x4, starting transfers between devices, swapped(): return lax.ppermute(value, 'parts', [(i, partner(i)) for i in range(count)])  24.3 us
    all_to_all x1, blocking collectives, step(): sums = lax.all_to_all(sums, 'parts', 0, 0, axis_index_groups=near)  16.5 us
    pallas_call x5, Pallas kernels, call(): pl.pallas_call(kernel, out_shape=[s if isinstance(s, jax.ShapeDtypeStruct...  8.86 us
    all_to_all x1, waiting for transfers between devices, step(): sums = lax.all_to_all(sums, 'parts', 0, 0, axis_index_groups=far)  5.65 us
    all_to_all x1, starting transfers between devices, step(): sums = lax.all_to_all(sums, 'parts', 0, 0, axis_index_groups=far)  3.92 us
  transfers between devices with their start and end apart: 5, of which 2 were waited for; matrix products, arithmetic and copies ran while one was open for 0% of the time, Pallas kernels for 5%

profile of v4, /device:TPU:1, one launch (start us, length us, event | category | flops | bytes accessed | tf_op | source)
XLA Modules:
  0.0 62.0 jit_solution(14504616517193962876)
XLA Ops:
  0.6 1.7 %shard_map.139 = (f32[160,128]{1,0:T(8,128)S(1)}, f32[160,128]{1,0:T(8,128)S(1)}, f32[48,128]{1,0:T(8,128)S(1)}, f32[48,128]{1,0:T(8,128)S(1)}, s32[1,51]{1,0:T(...) custom-call(f32[5,64,64]{2,1,0:T(8,128)} %flow_ref.1, f32[5,64,64]{2,1,0:T(8,128)} %tangent_ref.1, ...), custom_call_target="tpu_custom_call" | custom-call | tf_op jit(solution)/shard_map/pallas_call | solution.py:832
  2.3 8.7 %collective-permute-start = (f32[160,128]{1,0:T(8,128)S(1)}, f32[160,128]{1,0:T(8,128)S(1)}, u32[]{:S(2)}, u32[]{:S(2)}) collective-permute-start(f32[160,128]{1,0:T(8,128)S(1)} %get-tuple-element.29.sent_a_ref), channel_id=1, source_target_pairs={{0,1},{1,0},{2,3},{3,2},{4,5},{5,4},{6,7},{7,6},{8,9},{9,8},{10,11... | collective-permute-start | bytes 245768 | tf_op jit(solution)/shard_map/ppermute | solution.py:856
  11.1 1.9 %collective-permute-start.1 = (f32[160,128]{1,0:T(8,128)S(1)}, f32[160,128]{1,0:T(8,128)S(1)}, u32[]{:S(2)}, u32[]{:S(2)}) collective-permute-start(f32[160,128]{1,0:T(8,128)S(1)} %get-tuple-element.30.sent_b_ref), channel_id=1, source_target_pairs={{0,511},{1,2},{2,1},{3,4},{4,3},{5,6},{6,5},{7,8},{8,7},{9,10},{10... | collective-permute-start | bytes 245768 | tf_op jit(solution)/shard_map/ppermute | solution.py:856
  13.0 1.9 %collective-permute-start.2 = (f32[48,128]{1,0:T(8,128)S(1)}, f32[48,128]{1,0:T(8,128)S(1)}, u32[]{:S(2)}, u32[]{:S(2)}) collective-permute-start(f32[48,128]{1,0:T(8,128)S(1)} %get-tuple-element.35), channel_id=1, source_target_pairs={{0,2},{1,3},{2,0},{3,1},{4,6},{5,7},{6,4},{7,5},{8,10},{9,11},{10,... | collective-permute-start | bytes 73736 | tf_op jit(solution)/shard_map/ppermute | solution.py:856
  15.0 11.8 %collective-permute-start.3 = (f32[48,128]{1,0:T(8,128)S(1)}, f32[48,128]{1,0:T(8,128)S(1)}, u32[]{:S(2)}, u32[]{:S(2)}) collective-permute-start(f32[48,128]{1,0:T(8,128)S(1)} %get-tuple-element.36), channel_id=1, source_target_pairs={{0,510},{1,511},{2,4},{3,5},{4,2},{5,3},{6,8},{7,9},{8,6},{9,7},{1... | collective-permute-start | bytes 73736 | tf_op jit(solution)/shard_map/ppermute | solution.py:856
  26.7 0.0 collective-permute-done.2.c_ref
  26.7 1.2 %collective-permute-done.3.d_ref = f32[48,128]{1,0:T(8,128)S(1)} collective-permute-done((f32[48,128]{1,0:T(8,128)S(1)}, f32[48,128]{1,0:T(8,128)S(1)}, u32[]{:S(2)}, u32[]{:S(2)}) %collective-permute-start.3) | collective-permute-done | bytes 24608 | tf_op jit(solution)/shard_map/ppermute | solution.py:856
  27.9 0.0 collective-permute-done.a_ref
  27.9 0.0 collective-permute-done.1.b_ref
  27.9 0.0 copy-start.1
  27.9 3.5 %shard_map.142 = (f32[3,128]{1,0:T(4,128)S(1)}, f32[16,1,128]{2,1,0:T(1,128)S(1)}) custom-call(f32[160,128]{1,0:T(8,128)S(1)} %collective-permute-done.a_ref, f32[160,128]{1,0:T(8,128)S(1)} %collective-permute-done.1.b_ref, f32[48,128]{1,0:T(8,128)S(1)} %collective-permute-done.2.c_ref, f32[48,128]{1,0:T(8,128)S(1)} %collective-permute-done.3.d_ref, ...), custom_call_target="tpu_custom_call" | custom-call | tf_op jit(solution)/shard_map/pallas_call | solution.py:832
  31.4 16.5 %all_to_all.10 = f32[16,1,128]{2,1,0:T(1,128)S(1)} all-to-all(f32[16,1,128]{2,1,0:T(1,128)S(1)} %get-tuple-element.39), channel_id=1, replica_groups={{0,1,2,3,4,5,6,7,8,9,10,11,12,13,14,15},{16,17,18,19,20,21,22,23,24,25,..., dimensions={0} | all-to-all | bytes 16384 | tf_op jit(solution)/shard_map/all_to_all | solution.py:991
  48.0 0.6 broadcast_in_dim.2
  48.6 3.9 %all-to-all-start.1 = ((f32[32,1,128]{2,1,0:T(1,128)}), f32[32,1,128]{2,1,0:T(1,128)S(1)}, u32[]{:S(2)}, u32[]{:S(2)}) async-start(f32[32,1,128]{2,1,0:T(1,128)} %broadcast_in_dim.2), calls=%async_computation.1 | async-start | bytes 32768 | tf_op jit(solution)/shard_map/all_to_all | solution.py:994
  52.6 0.0 copy-done
  52.6 0.0 copy-done.1
  52.6 0.0 copy-done.2
  52.6 0.0 copy-done.3
  52.6 0.0 copy-done.4
  52.6 0.0 copy-done.5
  52.6 0.6 shard_map.140
  53.2 2.4 %shard_map.141 = (f32[5,64,64]{2,1,0:T(8,128)}, f32[5,64,64]{2,1,0:T(8,128)}) custom-call(f32[10,48,128]{2,1,0:T(8,128)S(1)} %get-tuple-element.23.inner_ref, f32[10,32,128]{2,1,0:T(8,128)S(1)} %get-tuple-element.24.state_ref, f32[10,48,128]{2,1,0:T(8,128)S(1)} %get-tuple-element.25.local_ref, f32[8,128]{1,0:T(8,128)S(1)} %get-tuple-element.26.places_ref, ...), custom_call_target="tpu_custom_call" | custom-call | flops 200000000 | bytes 1000000 | tf_op jit(solution)/shard_map/pallas_call | solution.py:832
  55.6 5.6 %all-to-all-done.1.sums_ref = f32[32,1,128]{2,1,0:T(1,128)S(1)} async-done(((f32[32,1,128]{2,1,0:T(1,128)}), f32[32,1,128]{2,1,0:T(1,128)S(1)}, u32[]{:S(2)}, u32[]{:S(2)}) %all-to-all-start.1) | async-done | bytes 16416 | tf_op jit(solution)/shard_map/all_to_all | solution.py:994
  61.2 0.7 %shard_map.143 = f32[3,102]{1,0:T(4,128)} custom-call(f32[32,1,128]{2,1,0:T(1,128)S(1)} %all-to-all-done.1.sums_ref, f32[3,128]{1,0:T(4,128)S(1)} %get-tuple-element.40.descent_ref), custom_call_target="tpu_custom_call" | custom-call | tf_op jit(solution)/shard_map/pallas_call | solution.py:832
  (6 shorter events, 0.0 us)
Async XLA Ops:
  2.3 25.6 %collective-permute-start = (f32[160,128]{1,0:T(8,128)S(1)}, f32[160,128]{1,0:T(8,128)S(1)}, u32[]{:S(2)}, u32[]{:S(2)}) collective-permute-start(f32[160,128]{1,0:T(8,128)S(1)} %get-tuple-element.29.sent_a_ref), channel_id=1, source_target_pairs={{0,1},{1,0},{2,3},{3,2},{4,5},{5,4},{6,7},{7,6},{8,9},{9,8},{10,11... | collective-permute-start | bytes 245768 | tf_op jit(solution)/shard_map/ppermute | solution.py:856
  11.1 16.8 %collective-permute-start.1 = (f32[160,128]{1,0:T(8,128)S(1)}, f32[160,128]{1,0:T(8,128)S(1)}, u32[]{:S(2)}, u32[]{:S(2)}) collective-permute-start(f32[160,128]{1,0:T(8,128)S(1)} %get-tuple-element.30.sent_b_ref), channel_id=1, source_target_pairs={{0,511},{1,2},{2,1},{3,4},{4,3},{5,6},{6,5},{7,8},{8,7},{9,10},{10... | collective-permute-start | bytes 245768 | tf_op jit(solution)/shard_map/ppermute | solution.py:856
  13.0 13.7 %collective-permute-start.2 = (f32[48,128]{1,0:T(8,128)S(1)}, f32[48,128]{1,0:T(8,128)S(1)}, u32[]{:S(2)}, u32[]{:S(2)}) collective-permute-start(f32[48,128]{1,0:T(8,128)S(1)} %get-tuple-element.35), channel_id=1, source_target_pairs={{0,2},{1,3},{2,0},{3,1},{4,6},{5,7},{6,4},{7,5},{8,10},{9,11},{10,... | collective-permute-start | bytes 73736 | tf_op jit(solution)/shard_map/ppermute | solution.py:856
  15.0 13.0 %collective-permute-start.3 = (f32[48,128]{1,0:T(8,128)S(1)}, f32[48,128]{1,0:T(8,128)S(1)}, u32[]{:S(2)}, u32[]{:S(2)}) collective-permute-start(f32[48,128]{1,0:T(8,128)S(1)} %get-tuple-element.36), channel_id=1, source_target_pairs={{0,510},{1,511},{2,4},{3,5},{4,2},{5,3},{6,8},{7,9},{8,6},{9,7},{1... | collective-permute-start | bytes 73736 | tf_op jit(solution)/shard_map/ppermute | solution.py:856
  27.9 24.6 %copy-start = (f32[5,64,64]{2,1,0:T(8,128)S(1)}, f32[5,64,64]{2,1,0:T(8,128)}, u32[]{:S(2)}) copy-start(f32[5,64,64]{2,1,0:T(8,128)} %flow_ref.1) | copy-start | bytes 245764
  27.9 24.6 %copy-start.1 = (f32[5,64,64]{2,1,0:T(8,128)S(1)}, f32[5,64,64]{2,1,0:T(8,128)}, u32[]{:S(2)}) copy-start(f32[5,64,64]{2,1,0:T(8,128)} %tangent_ref.1) | copy-start | bytes 245764
  48.6 4.0 %copy-start.2 = (s32[6,64]{1,0:T(8,128)S(1)}, s32[6,64]{1,0:T(8,128)}, u32[]{:S(2)}) copy-start(s32[6,64]{1,0:T(8,128)} %neighbour_ref.1) | copy-start | bytes 4612
  48.6 4.0 %copy-start.3 = (s32[8,64]{1,0:T(8,128)S(1)}, s32[8,64]{1,0:T(8,128)}, u32[]{:S(2)}) copy-start(s32[8,64]{1,0:T(8,128)} %nodes_ref.1) | copy-start | bytes 6148
  48.6 4.0 %copy-start.4 = (f32[3,102]{1,0:T(4,128)S(1)}, f32[3,102]{1,0:T(4,128)}, u32[]{:S(2)}) copy-start(f32[3,102]{1,0:T(4,128)} %places_ref.1) | copy-start | bytes 3676
  48.6 4.0 %copy-start.5 = (f32[5]{0:T(128)S(1)}, f32[5]{0:T(128)}, u32[]{:S(2)}) copy-start(f32[5]{0:T(128)} %param.14) | copy-start | bytes 64
  48.6 12.6 %all-to-all-start.1 = ((f32[32,1,128]{2,1,0:T(1,128)}), f32[32,1,128]{2,1,0:T(1,128)S(1)}, u32[]{:S(2)}, u32[]{:S(2)}) async-start(f32[32,1,128]{2,1,0:T(1,128)} %broadcast_in_dim.2), calls=%async_computation.1 | async-start | bytes 32768 | tf_op jit(solution)/shard_map/all_to_all | solution.py:994
